TPU v7x, 128 devices: a whole 4x4x4 slice. The times are simulated.
128 devices in a mesh: gx: 4 (over z), gy: 4 (over y), gz: 8 (over x, core).
Axes of the slice: x: 4, y: 4, z: 4, core: 2. Of those that a mesh axis runs over, the one named last changes fastest.
Arguments:
- basis: float32 [4, 64, 64, 64, 512], P(None, None, 'gz', 'gx', 'gy'), may hold values from -1000 to 1000
- stand_id: int32 [64, 64, 512], P('gz', 'gx', 'gy'), may hold values from 0 to 63
- drag_table: float32 [64], replicated, may hold values from 0.5 to 8
- stand_mask: int32 [64], replicated, may hold values 0 or 1
Outputs:
- fresh_block: float32 [64, 64, 64, 512], P(None, 'gz', 'gx', 'gy')
- projections: float32 [4, 64, 64], replicated
- factor: float32 [64, 64], replicated
All inputs are finite; a program needn't handle non-finite values.
Results may differ from a plain program's by a relative error of at most 0.00085.
Values sent between devices are 32-bit elements; how exact they have to be, the bound alone decides.
No kernel may reach another device: no remote copies, remote signals or barrier semaphores. Data moves between devices by JAX's collectives and lax.ppermute only.
A program may use at most 128 MiB of HBM per device.

v0:
```python
import jax
import jax.numpy as jnp
from jax import lax
from jax.experimental import pallas as pl
from jax.experimental.pallas import tpu as pltpu
from jax.sharding import PartitionSpec as P

advection = (0.3, 0.2, 0.1)
ROW_DIMS = (((1,), (1,)), ((), ()))
MAT_DIMS = (((1,), (0,)), ((), ()))
LANES = 128
F32 = jnp.float32
BF16 = jnp.bfloat16


def exchange(value, axis, mask):
    pairs = [(source, source ^ mask) for source in range(lax.axis_size(axis))]
    return lax.ppermute(value, axis, pairs)


def quad_sum(value, axis, masks):
    parts = [exchange(value, axis, mask) for mask in masks]
    return (value + parts[0]) + (parts[1] + parts[2])


def total(keep, give):
    part = keep + exchange(give, "gz", 1)
    part = quad_sum(part, "gz", (2, 4, 6))
    part = quad_sum(part, "gy", (1, 2, 3))
    part = quad_sum(part, "gx", (1, 2, 3))
    return part, exchange(part, "gz", 1)


def exact(left, right, numbers=MAT_DIMS):
    return lax.dot_general(left, right, numbers, precision=lax.Precision.HIGHEST, preferred_element_type=F32)


def narrow(left, right, numbers=MAT_DIMS):
    return lax.dot_general(left, right, numbers, preferred_element_type=F32)


def split(value):
    high = value.astype(BF16)
    return high, (value - high.astype(F32)).astype(BF16)


def resident(value):
    return pltpu.with_memory_space_constraint(value, pltpu.VMEM)


def even_here(axis, shape):
    return jnp.full(shape, lax.axis_index(axis) % 2, jnp.int32) == 0


def local_part(basis, stand_id, drag_table, stand_mask):
    rows, sx, sy, _ = basis.shape
    columns = rows // 4
    cells = sx * sy
    stands = drag_table.shape[0]
    slots = 3

    def kernel(table_in, mask_in, ids_in, src, halves, applied, own, xa, xb, ya, yb, za, zb, stage, newest, acc, table, mask, ids, sem, sems):
        def copy(x):
            return pltpu.make_async_copy(src.at[:, x], stage.at[x % slots], sem.at[x % slots])

        def at(cell):
            return newest[:, cell * LANES : (cell + 1) * LANES]

        small = [
            pltpu.make_async_copy(table_in, table, sems.at[0]),
            pltpu.make_async_copy(mask_in, mask, sems.at[1]),
            pltpu.make_async_copy(ids_in, ids, sems.at[2]),
        ]
        for item in small:
            item.start()
        for x in range(slots):
            copy(x).start()
        for item in small:
            item.wait()
        lane = lax.broadcasted_iota(jnp.int32, (columns, LANES), 1)
        one = lax.broadcasted_iota(jnp.int32, (1, LANES), 1)
        z_up = jnp.where(one == LANES - 1, 0.0, 1.0 + advection[2])
        z_down = jnp.where(one == 0, 0.0, 1.0 - advection[2])
        first = jnp.zeros((columns, LANES), F32)
        last = jnp.zeros((columns, LANES), F32)

        def apply(x, first, last):
            stand = ids[x]
            drag = jnp.zeros(stand.shape, F32)
            for s in range(stands):
                drag = jnp.where(stand == s, table[s] * mask[s].astype(F32), drag)
            for y in range(sy):
                cell = x * sy + y
                centre = at(cell)
                out = (6.0 + drag[y : y + 1, :]) * centre
                if x < sx - 1:
                    out = out - (1.0 + advection[0]) * at(cell + sy)
                if x > 0:
                    out = out - (1.0 - advection[0]) * at(cell - sy)
                if y < sy - 1:
                    out = out - (1.0 + advection[1]) * at(cell + 1)
                if y > 0:
                    out = out - (1.0 - advection[1]) * at(cell - 1)
                out = out - z_up * pltpu.roll(centre, LANES - 1, 1)
                out = out - z_down * pltpu.roll(centre, 1, 1)
                applied[:, cell * LANES : (cell + 1) * LANES] = out
                turned = pltpu.roll(centre, cell, 1) if cell else centre
                first = jnp.where(lane == cell, turned, first)
                last = jnp.where(lane == (cell - 1) % LANES, turned, last)
            return first, last

        for x in range(sx):
            copy(x).wait()
            for group in range(0, sy, 8):
                for base in range(0, rows, 32):
                    turned = pltpu.einshape("jyl->yjl", stage[x % slots, base : base + 32, group : group + 8, :])
                    for y in range(8):
                        cell = x * sy + group + y
                        cols = slice(cell * LANES, (cell + 1) * LANES)
                        high, low = split(turned[y])
                        halves[base : base + 32, cols] = high
                        halves[rows + base : rows + base + 32, cols] = low
                        if base >= rows - columns:
                            place = base - (rows - columns)
                            newest[place : place + 32, cols] = turned[y]
            if x + slots < sx:
                copy(x + slots).start()
            cols = slice(x * sy * LANES, (x + 1) * sy * LANES)
            gram = narrow(halves[:, cols], halves[0:rows, cols], ROW_DIMS)
            if x == 0:
                acc[...] = gram
            else:
                acc[...] += gram
            if x > 0:
                first, last = apply(x - 1, first, last)
        first, last = apply(sx - 1, first, last)
        even = even_here("gz", (columns, LANES))
        for y in range(sy):
            low, high = at(y), at((sx - 1) * sy + y)
            xa[y] = jnp.where(even, high, low)
            xb[y] = jnp.where(even, low, high)
        even = even_here("gx", (columns, LANES))
        for x in range(sx):
            low, high = at(x * sy), at(x * sy + sy - 1)
            ya[x] = jnp.where(even, high, low)
            yb[x] = jnp.where(even, low, high)
        even = even_here("gy", (columns, LANES))
        za[...] = jnp.where(even, last, first)
        zb[...] = jnp.where(even, first, last)
        cross = acc[rows : 2 * rows, :]
        own[...] = acc[0:rows, :] + cross + cross.T

    vmem = pl.BlockSpec(memory_space=pltpu.VMEM)
    return pl.pallas_call(
        kernel,
        in_specs=[pl.BlockSpec(memory_space=pltpu.HBM)] * 4,
        out_specs=[vmem] * 9,
        out_shape=[
            pltpu.VMEM((2 * rows, cells * LANES), BF16),
            pltpu.VMEM((columns, cells * LANES), F32),
            pltpu.VMEM((rows, rows), F32),
            pltpu.VMEM((sy, columns, LANES), F32),
            pltpu.VMEM((sy, columns, LANES), F32),
            pltpu.VMEM((sx, columns, LANES), F32),
            pltpu.VMEM((sx, columns, LANES), F32),
            pltpu.VMEM((columns, LANES), F32),
            pltpu.VMEM((columns, LANES), F32),
        ],
        scratch_shapes=[
            pltpu.VMEM((slots, rows, sy, LANES), F32),
            pltpu.VMEM((columns, cells * LANES), F32),
            pltpu.VMEM((2 * rows, rows), F32),
            pltpu.SMEM((stands,), F32),
            pltpu.SMEM((stands,), jnp.int32),
            pltpu.VMEM(stand_id.shape, jnp.int32),
            pltpu.SemaphoreType.DMA((slots,)),
            pltpu.SemaphoreType.DMA((3,)),
        ],
        compiler_params=pltpu.CompilerParams(vmem_limit_bytes=16 * 2**20),
        name="local_part",
    )(*[pltpu.with_memory_space_constraint(v, pltpu.HBM) for v in (drag_table, stand_mask, stand_id, basis)])


def products(halves, applied, own, halos, scale, sx, sy):
    rows2, width = halves.shape
    rows = rows2 // 2
    columns = applied.shape[0]
    half = rows // 2
    size = rows + half + columns + 16
    chunks = 4

    def kernel(halves, applied, own, xa, xb, ya, yb, za, zb, both, keep, give, passed, packed):
        def sides(axis, weight, one, two):
            index = lax.axis_index(axis)
            even = even_here(axis, (columns, LANES))
            down = jnp.where(index == 0, 0.0, 1.0 - weight)
            up = jnp.where(index == lax.axis_size(axis) - 1, 0.0, 1.0 + weight)
            low = [down * jnp.where(even, b, a) for a, b in zip(one, two)]
            high = [up * jnp.where(even, a, b) for a, b in zip(one, two)]
            return low, high

        lane = lax.broadcasted_iota(jnp.int32, (columns, LANES), 1)
        (z_low,), (z_high,) = sides("gy", advection[2], [za[...]], [zb[...]])
        cross, square = None, None
        for x in range(sx):
            if x == 0 or x == sx - 1:
                x_low, x_high = sides("gz", advection[0], [xa[y] for y in range(sy)], [xb[y] for y in range(sy)])
            (y_low,), (y_high,) = sides("gx", advection[1], [ya[x]], [yb[x]])
            for y in range(sy):
                cell = x * sy + y
                cols = slice(cell * LANES, (cell + 1) * LANES)
                value = applied[:, cols]
                if x == 0:
                    value = value - x_low[y]
                if x == sx - 1:
                    value = value - x_high[y]
                if y == 0:
                    value = value - y_low
                if y == sy - 1:
                    value = value - y_high
                shift = (1 - cell) % LANES
                low = pltpu.roll(z_low, shift, 1) if shift else z_low
                shift = (LANES - 1 - cell) % LANES
                high = pltpu.roll(z_high, shift, 1) if shift else z_high
                edge = jnp.where(lane == 0, low, jnp.where(lane == LANES - 1, high, 0.0))
                top, rest = split(value - edge)
                both[0:columns, cols] = top
                both[columns:, cols] = rest
            if (x + 1) % (sx // chunks) == 0:
                cols = slice((x + 1 - sx // chunks) * sy * LANES, (x + 1) * sy * LANES)
                one = narrow(halves[:, cols], both[:, cols], ROW_DIMS)
                two = narrow(both[:, cols], both[:, cols], ROW_DIMS)
                cross = one if cross is None else cross + one
                square = two if square is None else square + two
        mixed = cross[0:rows, :] + cross[rows:, :]
        coeffs = (mixed[:, 0:columns] + mixed[:, columns:]) * scale
        square = square[0:columns, :] + square[columns:, :]
        square = (square[:, 0:columns] + square[:, columns:]) * scale
        corner = own[half:, half:] * scale
        row = lax.broadcasted_iota(jnp.int32, (half, half), 0)
        col = lax.broadcasted_iota(jnp.int32, (half, half), 1)
        packed[0:half, :] = own[0:half, half:] * scale
        packed[half:rows, :] = jnp.where(row <= col, own[0:half, 0:half] * scale, corner)
        packed[rows : rows + half, 0:columns] = coeffs[0:half, :]
        packed[rows : rows + half, columns:] = coeffs[half:, :]
        packed[rows + half : rows + half + columns, :] = jnp.zeros((columns, LANES), F32)
        packed[rows + half : rows + half + columns, 0:columns] = square
        diag = jnp.sum(jnp.where(row == col, corner, 0.0), axis=0, keepdims=True)
        packed[rows + half + columns :, :] = jnp.broadcast_to(diag, (16, LANES))
        core = lax.axis_index("gz") % 2
        part = size // 2
        keep[...] = packed[pl.ds(pl.multiple_of(core * part, 8), part), :]
        give[...] = packed[pl.ds(pl.multiple_of((1 - core) * part, 8), part), :]

    vmem = pl.BlockSpec(memory_space=pltpu.VMEM)
    return pl.pallas_call(
        kernel,
        in_specs=[vmem] * 9,
        out_specs=[vmem] * 4,
        out_shape=[
            pltpu.VMEM((2 * columns, width), BF16),
            pltpu.VMEM((size // 2, LANES), F32),
            pltpu.VMEM((size // 2, LANES), F32),
            pltpu.VMEM((rows2, width), BF16),
        ],
        input_output_aliases={0: 3},
        scratch_shapes=[pltpu.VMEM((size, LANES), F32)],
        compiler_params=pltpu.CompilerParams(vmem_limit_bytes=8 * 2**20),
        name="products",
    )(halves, applied, own, *[resident(h) for h in halos])


def finish(part, other, halves, applied, sx, sy):
    rows = halves.shape[0] // 2
    columns = applied.shape[0] // 2
    half = rows // 2
    width = sy * LANES
    size = part.shape[0]

    def kernel(part, other, basis, block, fresh, coeffs_out, factor_out, staged, packed, residual, sem_out):
        core = lax.axis_index("gz") % 2
        packed[pl.ds(pl.multiple_of(core * size, 8), size), :] = part[...]
        packed[pl.ds(pl.multiple_of((1 - core) * size, 8), size), :] = other[...]
        row = lax.broadcasted_iota(jnp.int32, (half, half), 0)
        col = lax.broadcasted_iota(jnp.int32, (half, half), 1)
        mixed = packed[half:rows, :]
        upper = jnp.where(row < col, mixed, 0.0)
        s11 = upper + upper.T + jnp.where(row == col, mixed, 0.0)
        lower = jnp.where(row > col, mixed, 0.0)
        diag = packed[rows + half + columns : rows + half + columns + 1, :]
        s22 = lower + lower.T + jnp.where(row == col, diag, 0.0)
        s12 = packed[0:half, :]
        coeffs = jnp.concatenate(
            [packed[rows : rows + half, 0:columns], packed[rows : rows + half, columns:]], axis=0
        )
        coeffs_out[...] = coeffs
        turned = coeffs.T
        left, right = turned[:, 0:half], turned[:, half:]
        first = exact(left, s11) + exact(right, s12, ROW_DIMS) - 2.0 * left
        second = exact(left, s12) + exact(right, s22) - 2.0 * right
        gram = packed[rows + half : rows + half + columns, 0:columns]
        gram = gram + exact(first, left, ROW_DIMS) + exact(second, right, ROW_DIMS)
        gram = 0.5 * (gram + gram.T)
        eye = (
            lax.broadcasted_iota(jnp.int32, (columns, columns), 0)
            == lax.broadcasted_iota(jnp.int32, (columns, columns), 1)
        ).astype(F32)
        work = jnp.concatenate([gram, eye], axis=1)
        turned_both = jnp.concatenate(split(turned), axis=0)
        tiles = [work[t : t + 8, :] for t in range(0, columns, 8)]
        sub = lax.broadcasted_iota(jnp.int32, (8, LANES), 0)
        piece = sx * width // columns
        for j in range(columns):
            pivot_tile = tiles[j // 8]
            pivot = pivot_tile[j % 8 : j % 8 + 1, j : j + 1]
            scaled = pivot_tile[j % 8 : j % 8 + 1, :] * (1.0 / pivot)
            for t in range(j // 8, columns // 8):
                times = jnp.broadcast_to(tiles[t][:, j : j + 1], (8, LANES))
                if t == j // 8:
                    times = jnp.where(sub > j % 8, times, 0.0)
                tiles[t] = tiles[t] - times * scaled
            cols = slice(j * piece, (j + 1) * piece)
            big = narrow(turned_both, basis[0:rows, cols])
            taken = big[0:columns] + big[columns:] + narrow(turned_both[0:columns], basis[rows:, cols])
            value = (block[0:columns, cols].astype(F32) - taken) + block[columns:, cols].astype(F32)
            high, low = split(value)
            residual[0:columns, cols] = high
            residual[columns:, cols] = low
        solved = jnp.concatenate(tiles, axis=0)
        tri_row = lax.broadcasted_iota(jnp.int32, (columns, LANES), 0)
        tri_col = lax.broadcasted_iota(jnp.int32, (columns, LANES), 1)
        pivots = jnp.sum(jnp.where(tri_row == tri_col, solved, 0.0), axis=1, keepdims=True)
        inverse = lax.rsqrt(pivots)
        inverse = inverse * (1.5 - 0.5 * pivots * inverse * inverse)
        solved = solved * inverse
        factor_out[...] = jnp.where(tri_row <= tri_col, solved, 0.0)[:, 0:columns]
        inv_both = jnp.concatenate(split(solved[:, columns:]), axis=0)
        outs = []
        for x in range(sx):
            cols = slice(x * width, (x + 1) * width)
            big = narrow(inv_both, residual[0:columns, cols])
            value = big[0:columns] + big[columns:] + narrow(inv_both[0:columns], residual[columns:, cols])
            slot = x % 2
            if x >= 2:
                outs[x - 2].wait()
            for group in range(0, sy, 8):
                rows_y = [value[:, (group + y) * LANES : (group + y + 1) * LANES][None] for y in range(8)]
                staged[slot, :, group : group + 8, :] = pltpu.einshape("yjl->jyl", jnp.concatenate(rows_y, axis=0))
            outs.append(pltpu.make_async_copy(staged.at[slot], fresh.at[:, x], sem_out.at[slot]))
            outs[x].start()
        outs[sx - 2].wait()
        outs[sx - 1].wait()

    vmem = pl.BlockSpec(memory_space=pltpu.VMEM)
    anywhere = pl.BlockSpec(memory_space=pl.ANY)
    return pl.pallas_call(
        kernel,
        in_specs=[vmem] * 4,
        out_specs=[anywhere, vmem, vmem],
        out_shape=[
            jax.ShapeDtypeStruct((columns, sx, sy, LANES), F32),
            jax.ShapeDtypeStruct((rows, columns), F32),
            jax.ShapeDtypeStruct((columns, columns), F32),
        ],
        scratch_shapes=[
            pltpu.VMEM((2, columns, sy, LANES), F32),
            pltpu.VMEM((2 * size, LANES), F32),
            pltpu.VMEM(applied.shape, BF16),
            pltpu.SemaphoreType.DMA((2,)),
        ],
        compiler_params=pltpu.CompilerParams(vmem_limit_bytes=14 * 2**20),
        name="finish",
    )(resident(part), resident(other), halves, applied)


def swap(one, two, axis):
    count = lax.axis_size(axis)
    near = [(i, i ^ 1) for i in range(count)]
    far = [(i, (i - 1) % count if i % 2 == 0 else (i + 1) % count) for i in range(count)]
    return lax.ppermute(one, axis, near), lax.ppermute(two, axis, far)


def body(basis, stand_id, drag_table, stand_mask):
    blocks, columns, sx, sy, sz = basis.shape
    ncells = sx * sy * sz * lax.axis_size("gx") * lax.axis_size("gy") * lax.axis_size("gz")
    halves, applied, own, xa, xb, ya, yb, za, zb = local_part(
        basis.reshape(blocks * columns, sx, sy, sz), stand_id, drag_table, stand_mask
    )
    halos = (*swap(xa, xb, "gz"), *swap(ya, yb, "gx"), *swap(za, zb, "gy"))
    applied, keep, give, halves = products(halves, applied, own, halos, 1.0 / ncells, sx, sy)
    part, other = total(keep, give)
    fresh_block, coeffs, factor = finish(part, other, halves, applied, sx, sy)
    return fresh_block, coeffs.reshape(blocks, columns, columns), factor


def solution(mesh):
    placed = (P(None, None, "gz", "gx", "gy"), P("gz", "gx", "gy"), P(), P())
    return jax.shard_map(
        body,
        mesh=mesh,
        in_specs=placed,
        out_specs=(P(None, "gz", "gx", "gy"), P(), P()),
        check_vma=False,
    )
```

profile of v0, /device:TPU:0, one launch (start us, length us, event | category | flops | bytes accessed | tf_op | source)
XLA Modules:
  0.0 82.1 jit_solution(12200947125928129580)
XLA Ops:
  0.6 15.6 %local_part.1 = (bf16[512,16384]{1,0:T(8,128)(2,1)S(1)}, f32[64,16384]{1,0:T(8,128)S(1)}, f32[256,256]{1,0:T(8,128)S(1)}, f32[16,64,128]{2,1,0:T(8,128)S(1)}, f3...) custom-call(f32[64]{0:T(128)} %table_in.1, ...), custom_call_target="tpu_custom_call" | custom-call | tf_op jit(solution)/shard_map/local_part/pallas_call | solution.py:154
  16.3 2.9 %collective-permute-start.1 = (f32[16,64,128]{2,1,0:T(8,128)S(1)}, f32[16,64,128]{2,1,0:T(8,128)S(1)}, u32[]{:S(2)}, u32[]{:S(2)}) collective-permute-start(f32[16,64,128]{2,1,0:T(8,128)S(1)} %get-tuple-element.23), channel_id=1, source_target_pairs={{0,7},{1,2},{2,1},{3,4},{4,3},{5,6},{6,5},{7,0},{8,15},{9,10},{10,... | collective-permute-start | bytes 1572872 | tf_op jit(solution)/shard_map/ppermute | solution.py:380
  19.3 1.9 %collective-permute-start.2 = (f32[8,64,128]{2,1,0:T(8,128)S(1)}, f32[8,64,128]{2,1,0:T(8,128)S(1)}, u32[]{:S(2)}, u32[]{:S(2)}) collective-permute-start(f32[8,64,128]{2,1,0:T(8,128)S(1)} %get-tuple-element.24), channel_id=1, source_target_pairs={{0,32},{32,0},{64,96},{96,64},{1,33},{33,1},{65,97},{97,65},{2,34}... | collective-permute-start | bytes 786440 | tf_op jit(solution)/shard_map/ppermute | solution.py:380
  21.2 2.5 %collective-permute-start.3 = (f32[8,64,128]{2,1,0:T(8,128)S(1)}, f32[8,64,128]{2,1,0:T(8,128)S(1)}, u32[]{:S(2)}, u32[]{:S(2)}) collective-permute-start(f32[8,64,128]{2,1,0:T(8,128)S(1)} %get-tuple-element.25), channel_id=1, source_target_pairs={{0,96},{32,64},{64,32},{96,0},{1,97},{33,65},{65,33},{97,1},{2,98}... | collective-permute-start | bytes 786440 | tf_op jit(solution)/shard_map/ppermute | solution.py:380
  23.7 1.6 %collective-permute-start.4 = (f32[64,128]{1,0:T(8,128)S(1)}, f32[64,128]{1,0:T(8,128)S(1)}, u32[]{:S(2)}, u32[]{:S(2)}) collective-permute-start(f32[64,128]{1,0:T(8,128)S(1)} %get-tuple-element.26), channel_id=1, source_target_pairs={{0,8},{8,0},{16,24},{24,16},{1,9},{9,1},{17,25},{25,17},{2,10},{10... | collective-permute-start | bytes 98312 | tf_op jit(solution)/shard_map/ppermute | solution.py:380
  25.3 2.3 %collective-permute-done.4.za = f32[64,128]{1,0:T(8,128)S(1)} collective-permute-done((f32[64,128]{1,0:T(8,128)S(1)}, f32[64,128]{1,0:T(8,128)S(1)}, u32[]{:S(2)}, u32[]{:S(2)}) %collective-permute-start.4) | collective-permute-done | bytes 32800 | tf_op jit(solution)/shard_map/ppermute | solution.py:380
  27.6 3.0 %collective-permute-start.5 = (f32[64,128]{1,0:T(8,128)S(1)}, f32[64,128]{1,0:T(8,128)S(1)}, u32[]{:S(2)}, u32[]{:S(2)}) collective-permute-start(f32[64,128]{1,0:T(8,128)S(1)} %get-tuple-element.27), channel_id=1, source_target_pairs={{0,24},{8,16},{16,8},{24,0},{1,25},{9,17},{17,9},{25,1},{2,26},{10... | collective-permute-start | bytes 98312 | tf_op jit(solution)/shard_map/ppermute | solution.py:380
  30.6 2.1 %collective-permute-done.5.zb = f32[64,128]{1,0:T(8,128)S(1)} collective-permute-done((f32[64,128]{1,0:T(8,128)S(1)}, f32[64,128]{1,0:T(8,128)S(1)}, u32[]{:S(2)}, u32[]{:S(2)}) %collective-permute-start.5) | collective-permute-done | bytes 32800 | tf_op jit(solution)/shard_map/ppermute | solution.py:380
  32.8 5.9 %products.1 = (bf16[128,16384]{1,0:T(8,128)(2,1)S(1)}, f32[232,128]{1,0:T(8,128)S(1)}, f32[232,128]{1,0:T(8,128)S(1)}, bf16[512,16384]{1,0:T(8,128)(2,1)S(1)}) custom-call(bf16[512,16384]{1,0:T(8,128)(2,1)S(1)} %get-tuple-element.19.halves, f32[64,16384]{1,0:T(8,128)S(1)} %get-tuple-element.20.applied, ...), custom_call_target="tpu_custom_call", output_to_operand_aliasing={{3}: (0, {})} | custom-call | tf_op jit(solution)/shard_map/products/pallas_call | solution.py:256
  38.7 1.3 %collective-permute-done.6 = f32[232,128]{1,0:T(8,128)S(1)} collective-permute-done((f32[232,128]{1,0:T(8,128)S(1)}, f32[232,128]{1,0:T(8,128)S(1)}, u32[]{:S(2)}, u32[]{:S(2)}) %collective-permute-start.6) | collective-permute-done | bytes 118816 | tf_op jit(solution)/shard_map/ppermute | solution.py:18
  40.1 0.9 %collective-permute-start.9 = (f32[232,128]{1,0:T(8,128)S(1)}, f32[232,128]{1,0:T(8,128)S(1)}, u32[]{:S(2)}, u32[]{:S(2)}) collective-permute-start(f32[232,128]{1,0:T(8,128)S(1)} %add.30), channel_id=1, source_target_pairs={{0,6},{1,7},{2,4},{3,5},{4,2},{5,3},{6,0},{7,1},{8,14},{9,15},{10,... | collective-permute-start | bytes 356360 | tf_op jit(solution)/shard_map/ppermute | solution.py:18
  41.5 2.7 %collective-permute-start.7 = (f32[232,128]{1,0:T(8,128)S(1)}, f32[232,128]{1,0:T(8,128)S(1)}, u32[]{:S(2)}, u32[]{:S(2)}) collective-permute-start(f32[232,128]{1,0:T(8,128)S(1)} %add.30), channel_id=1, source_target_pairs={{0,2},{1,3},{2,0},{3,1},{4,6},{5,7},{6,4},{7,5},{8,10},{9,11},{10,... | collective-permute-start | bytes 356360 | tf_op jit(solution)/shard_map/ppermute | solution.py:18
  44.2 4.9 %collective-permute-done.9 = f32[232,128]{1,0:T(8,128)S(1)} collective-permute-done((f32[232,128]{1,0:T(8,128)S(1)}, f32[232,128]{1,0:T(8,128)S(1)}, u32[]{:S(2)}, u32[]{:S(2)}) %collective-permute-start.9) | collective-permute-done | bytes 118816 | tf_op jit(solution)/shard_map/ppermute | solution.py:18
  49.9 3.1 %collective-permute-start.12 = (f32[232,128]{1,0:T(8,128)S(1)}, f32[232,128]{1,0:T(8,128)S(1)}, u32[]{:S(2)}, u32[]{:S(2)}) collective-permute-start(f32[232,128]{1,0:T(8,128)S(1)} %add_add_fusion.2), channel_id=1, source_target_pairs={{0,24},{8,16},{16,8},{24,0},{1,25},{9,17},{17,9},{25,1},{2,26},{10... | collective-permute-start | bytes 356360 | tf_op jit(solution)/shard_map/ppermute | solution.py:18
  52.9 1.1 %collective-permute-start.10 = (f32[232,128]{1,0:T(8,128)S(1)}, f32[232,128]{1,0:T(8,128)S(1)}, u32[]{:S(2)}, u32[]{:S(2)}) collective-permute-start(f32[232,128]{1,0:T(8,128)S(1)} %add_add_fusion.2), channel_id=1, source_target_pairs={{0,8},{8,0},{16,24},{24,16},{1,9},{9,1},{17,25},{25,17},{2,10},{10... | collective-permute-start | bytes 356360 | tf_op jit(solution)/shard_map/ppermute | solution.py:18
  54.0 3.2 %collective-permute-done.12 = f32[232,128]{1,0:T(8,128)S(1)} collective-permute-done((f32[232,128]{1,0:T(8,128)S(1)}, f32[232,128]{1,0:T(8,128)S(1)}, u32[]{:S(2)}, u32[]{:S(2)}) %collective-permute-start.12) | collective-permute-done | bytes 118816 | tf_op jit(solution)/shard_map/ppermute | solution.py:18
  57.3 2.4 %collective-permute-done.11 = f32[232,128]{1,0:T(8,128)S(1)} collective-permute-done((f32[232,128]{1,0:T(8,128)S(1)}, f32[232,128]{1,0:T(8,128)S(1)}, u32[]{:S(2)}, u32[]{:S(2)}) %collective-permute-start.11) | collective-permute-done | bytes 118816 | tf_op jit(solution)/shard_map/ppermute | solution.py:18
  59.7 0.8 collective-permute-start.15
  60.5 2.4 %collective-permute-start.14 = (f32[232,128]{1,0:T(8,128)S(1)}, f32[232,128]{1,0:T(8,128)S(1)}, u32[]{:S(2)}, u32[]{:S(2)}) collective-permute-start(f32[232,128]{1,0:T(8,128)S(1)} %add_add_fusion.1), channel_id=1, source_target_pairs={{0,64},{32,96},{64,0},{96,32},{1,65},{33,97},{65,1},{97,33},{2,66}... | collective-permute-start | bytes 356360 | tf_op jit(solution)/shard_map/ppermute | solution.py:18
  62.9 1.0 %collective-permute-start.13 = (f32[232,128]{1,0:T(8,128)S(1)}, f32[232,128]{1,0:T(8,128)S(1)}, u32[]{:S(2)}, u32[]{:S(2)}) collective-permute-start(f32[232,128]{1,0:T(8,128)S(1)} %add_add_fusion.1), channel_id=1, source_target_pairs={{0,32},{32,0},{64,96},{96,64},{1,33},{33,1},{65,97},{97,65},{2,34}... | collective-permute-start | bytes 356360 | tf_op jit(solution)/shard_map/ppermute | solution.py:18
  63.9 3.2 %collective-permute-done.15 = f32[232,128]{1,0:T(8,128)S(1)} collective-permute-done((f32[232,128]{1,0:T(8,128)S(1)}, f32[232,128]{1,0:T(8,128)S(1)}, u32[]{:S(2)}, u32[]{:S(2)}) %collective-permute-start.15) | collective-permute-done | bytes 118816 | tf_op jit(solution)/shard_map/ppermute | solution.py:18
  67.1 0.9 %collective-permute-done.13 = f32[232,128]{1,0:T(8,128)S(1)} collective-permute-done((f32[232,128]{1,0:T(8,128)S(1)}, f32[232,128]{1,0:T(8,128)S(1)}, u32[]{:S(2)}, u32[]{:S(2)}) %collective-permute-start.13) | collective-permute-done | bytes 118816 | tf_op jit(solution)/shard_map/ppermute | solution.py:18
  68.3 1.3 %collective-permute-done.16.other = f32[232,128]{1,0:T(8,128)S(1)} collective-permute-done((f32[232,128]{1,0:T(8,128)S(1)}, f32[232,128]{1,0:T(8,128)S(1)}, u32[]{:S(2)}, u32[]{:S(2)}) %collective-permute-start.16) | collective-permute-done | bytes 118816 | tf_op jit(solution)/shard_map/ppermute | solution.py:18
  69.6 12.3 %finish.1 = (f32[64,8,16,128]{3,2,1,0:T(8,128)}, f32[256,64]{1,0:T(8,128)}, f32[64,64]{1,0:T(8,128)}) custom-call(f32[232,128]{1,0:T(8,128)S(1)} %add_add_fusion.part, f32[232,128]{1,0:T(8,128)S(1)} %collective-permute-done.16.other, bf16[512,16384]{1,0:T(8,128)(2,1)S(1)} %get-tuple-element.30.basis, bf16[128,16384]{1,0:T(8,128)(2,1)S(1)} %get-tuple-element.31.block), custom_call_target="tpu_custom_call" | custom-call | tf_op jit(solution)/shard_map/finish/pallas_call | solution.py:356
  (17 shorter events, 1.8 us)
Async XLA Ops:
  16.2 16.5 %collective-permute-start = (f32[16,64,128]{2,1,0:T(8,128)S(1)}, f32[16,64,128]{2,1,0:T(8,128)S(1)}, u32[]{:S(2)}, u32[]{:S(2)}) collective-permute-start(f32[16,64,128]{2,1,0:T(8,128)S(1)} %get-tuple-element.22), channel_id=1, source_target_pairs={{0,1},{1,0},{2,3},{3,2},{4,5},{5,4},{6,7},{7,6},{8,9},{9,8},{10,11... | collective-permute-start | bytes 1572872 | tf_op jit(solution)/shard_map/ppermute | solution.py:380
  16.3 16.4 %collective-permute-start.1 = (f32[16,64,128]{2,1,0:T(8,128)S(1)}, f32[16,64,128]{2,1,0:T(8,128)S(1)}, u32[]{:S(2)}, u32[]{:S(2)}) collective-permute-start(f32[16,64,128]{2,1,0:T(8,128)S(1)} %get-tuple-element.23), channel_id=1, source_target_pairs={{0,7},{1,2},{2,1},{3,4},{4,3},{5,6},{6,5},{7,0},{8,15},{9,10},{10,... | collective-permute-start | bytes 1572872 | tf_op jit(solution)/shard_map/ppermute | solution.py:380
  19.3 13.5 %collective-permute-start.2 = (f32[8,64,128]{2,1,0:T(8,128)S(1)}, f32[8,64,128]{2,1,0:T(8,128)S(1)}, u32[]{:S(2)}, u32[]{:S(2)}) collective-permute-start(f32[8,64,128]{2,1,0:T(8,128)S(1)} %get-tuple-element.24), channel_id=1, source_target_pairs={{0,32},{32,0},{64,96},{96,64},{1,33},{33,1},{65,97},{97,65},{2,34}... | collective-permute-start | bytes 786440 | tf_op jit(solution)/shard_map/ppermute | solution.py:380
  21.2 11.6 %collective-permute-start.3 = (f32[8,64,128]{2,1,0:T(8,128)S(1)}, f32[8,64,128]{2,1,0:T(8,128)S(1)}, u32[]{:S(2)}, u32[]{:S(2)}) collective-permute-start(f32[8,64,128]{2,1,0:T(8,128)S(1)} %get-tuple-element.25), channel_id=1, source_target_pairs={{0,96},{32,64},{64,32},{96,0},{1,97},{33,65},{65,33},{97,1},{2,98}... | collective-permute-start | bytes 786440 | tf_op jit(solution)/shard_map/ppermute | solution.py:380
  23.7 3.9 %collective-permute-start.4 = (f32[64,128]{1,0:T(8,128)S(1)}, f32[64,128]{1,0:T(8,128)S(1)}, u32[]{:S(2)}, u32[]{:S(2)}) collective-permute-start(f32[64,128]{1,0:T(8,128)S(1)} %get-tuple-element.26), channel_id=1, source_target_pairs={{0,8},{8,0},{16,24},{24,16},{1,9},{9,1},{17,25},{25,17},{2,10},{10... | collective-permute-start | bytes 98312 | tf_op jit(solution)/shard_map/ppermute | solution.py:380
  27.6 5.1 %collective-permute-start.5 = (f32[64,128]{1,0:T(8,128)S(1)}, f32[64,128]{1,0:T(8,128)S(1)}, u32[]{:S(2)}, u32[]{:S(2)}) collective-permute-start(f32[64,128]{1,0:T(8,128)S(1)} %get-tuple-element.27), channel_id=1, source_target_pairs={{0,24},{8,16},{16,8},{24,0},{1,25},{9,17},{17,9},{25,1},{2,26},{10... | collective-permute-start | bytes 98312 | tf_op jit(solution)/shard_map/ppermute | solution.py:380
  38.6 1.4 %collective-permute-start.6 = (f32[232,128]{1,0:T(8,128)S(1)}, f32[232,128]{1,0:T(8,128)S(1)}, u32[]{:S(2)}, u32[]{:S(2)}) collective-permute-start(f32[232,128]{1,0:T(8,128)S(1)} %get-tuple-element.29), channel_id=1, source_target_pairs={{0,1},{1,0},{2,3},{3,2},{4,5},{5,4},{6,7},{7,6},{8,9},{9,8},{10,11... | collective-permute-start | bytes 356360 | tf_op jit(solution)/shard_map/ppermute | solution.py:18
  40.1 9.1 %collective-permute-start.9 = (f32[232,128]{1,0:T(8,128)S(1)}, f32[232,128]{1,0:T(8,128)S(1)}, u32[]{:S(2)}, u32[]{:S(2)}) collective-permute-start(f32[232,128]{1,0:T(8,128)S(1)} %add.30), channel_id=1, source_target_pairs={{0,6},{1,7},{2,4},{3,5},{4,2},{5,3},{6,0},{7,1},{8,14},{9,15},{10,... | collective-permute-start | bytes 356360 | tf_op jit(solution)/shard_map/ppermute | solution.py:18
  41.0 8.2 %collective-permute-start.8 = (f32[232,128]{1,0:T(8,128)S(1)}, f32[232,128]{1,0:T(8,128)S(1)}, u32[]{:S(2)}, u32[]{:S(2)}) collective-permute-start(f32[232,128]{1,0:T(8,128)S(1)} %add.30), channel_id=1, source_target_pairs={{0,4},{1,5},{2,6},{3,7},{4,0},{5,1},{6,2},{7,3},{8,12},{9,13},{10,... | collective-permute-start | bytes 356360 | tf_op jit(solution)/shard_map/ppermute | solution.py:18
  41.5 8.3 %collective-permute-start.7 = (f32[232,128]{1,0:T(8,128)S(1)}, f32[232,128]{1,0:T(8,128)S(1)}, u32[]{:S(2)}, u32[]{:S(2)}) collective-permute-start(f32[232,128]{1,0:T(8,128)S(1)} %add.30), channel_id=1, source_target_pairs={{0,2},{1,3},{2,0},{3,1},{4,6},{5,7},{6,4},{7,5},{8,10},{9,11},{10,... | collective-permute-start | bytes 356360 | tf_op jit(solution)/shard_map/ppermute | solution.py:18
  49.9 7.4 %collective-permute-start.12 = (f32[232,128]{1,0:T(8,128)S(1)}, f32[232,128]{1,0:T(8,128)S(1)}, u32[]{:S(2)}, u32[]{:S(2)}) collective-permute-start(f32[232,128]{1,0:T(8,128)S(1)} %add_add_fusion.2), channel_id=1, source_target_pairs={{0,24},{8,16},{16,8},{24,0},{1,25},{9,17},{17,9},{25,1},{2,26},{10... | collective-permute-start | bytes 356360 | tf_op jit(solution)/shard_map/ppermute | solution.py:18
  52.9 6.7 %collective-permute-start.11 = (f32[232,128]{1,0:T(8,128)S(1)}, f32[232,128]{1,0:T(8,128)S(1)}, u32[]{:S(2)}, u32[]{:S(2)}) collective-permute-start(f32[232,128]{1,0:T(8,128)S(1)} %add_add_fusion.2), channel_id=1, source_target_pairs={{0,16},{8,24},{16,0},{24,8},{1,17},{9,25},{17,1},{25,9},{2,18},{10... | collective-permute-start | bytes 356360 | tf_op jit(solution)/shard_map/ppermute | solution.py:18
  52.9 6.7 %collective-permute-start.10 = (f32[232,128]{1,0:T(8,128)S(1)}, f32[232,128]{1,0:T(8,128)S(1)}, u32[]{:S(2)}, u32[]{:S(2)}) collective-permute-start(f32[232,128]{1,0:T(8,128)S(1)} %add_add_fusion.2), channel_id=1, source_target_pairs={{0,8},{8,0},{16,24},{24,16},{1,9},{9,1},{17,25},{25,17},{2,10},{10... | collective-permute-start | bytes 356360 | tf_op jit(solution)/shard_map/ppermute | solution.py:18
  59.7 7.4 %collective-permute-start.15 = (f32[232,128]{1,0:T(8,128)S(1)}, f32[232,128]{1,0:T(8,128)S(1)}, u32[]{:S(2)}, u32[]{:S(2)}) collective-permute-start(f32[232,128]{1,0:T(8,128)S(1)} %add_add_fusion.1), channel_id=1, source_target_pairs={{0,96},{32,64},{64,32},{96,0},{1,97},{33,65},{65,33},{97,1},{2,98}... | collective-permute-start | bytes 356360 | tf_op jit(solution)/shard_map/ppermute | solution.py:18
  60.5 6.6 %collective-permute-start.14 = (f32[232,128]{1,0:T(8,128)S(1)}, f32[232,128]{1,0:T(8,128)S(1)}, u32[]{:S(2)}, u32[]{:S(2)}) collective-permute-start(f32[232,128]{1,0:T(8,128)S(1)} %add_add_fusion.1), channel_id=1, source_target_pairs={{0,64},{32,96},{64,0},{96,32},{1,65},{33,97},{65,1},{97,33},{2,66}... | collective-permute-start | bytes 356360 | tf_op jit(solution)/shard_map/ppermute | solution.py:18
  62.9 5.1 %collective-permute-start.13 = (f32[232,128]{1,0:T(8,128)S(1)}, f32[232,128]{1,0:T(8,128)S(1)}, u32[]{:S(2)}, u32[]{:S(2)}) collective-permute-start(f32[232,128]{1,0:T(8,128)S(1)} %add_add_fusion.1), channel_id=1, source_target_pairs={{0,32},{32,0},{64,96},{96,64},{1,33},{33,1},{65,97},{97,65},{2,34}... | collective-permute-start | bytes 356360 | tf_op jit(solution)/shard_map/ppermute | solution.py:18
  68.0 1.6 %collective-permute-start.16 = (f32[232,128]{1,0:T(8,128)S(1)}, f32[232,128]{1,0:T(8,128)S(1)}, u32[]{:S(2)}, u32[]{:S(2)}) collective-permute-start(f32[232,128]{1,0:T(8,128)S(1)} %add_add_fusion.part), channel_id=1, source_target_pairs={{0,1},{1,0},{2,3},{3,2},{4,5},{5,4},{6,7},{7,6},{8,9},{9,8},{10,11... | collective-permute-start | bytes 356360 | tf_op jit(solution)/shard_map/ppermute | solution.py:18
where the time goes:
time: 83.2 us; the launch traced here: 82.1 us
  Pallas kernels  33.7 us (41%)
  starting transfers between devices  25 us (30%)
  waiting for transfers between devices  22.4 us (27%)
  between operations  0.89 us (1%)
    ppermute x11, waiting for transfers between devices, exchange(): return lax.ppermute(value, axis, pairs)  17.9 us
    pallas_call x1, Pallas kernels, local_part(): pl.pallas_call(kernel, in_specs=[pl.BlockSpec(memory_space=pltpu.HBM)] *...  15.6 us
    ppermute x11, starting transfers between devices, exchange(): return lax.ppermute(value, axis, pairs)  12.9 us
    pallas_call x1, Pallas kernels, finish(): pl.pallas_call(kernel, in_specs=[vmem] * 4, out_specs=[anywhere, vmem, vm...  12.3 us
    ppermute x6, starting transfers between devices, swap(): return (lax.ppermute(one, axis, near), lax.ppermute(two, axis, far))  12.1 us
    pallas_call x1, Pallas kernels, products(): pl.pallas_call(kernel, in_specs=[vmem] * 9, out_specs=[vmem] * 4, out_sha...  5.87 us
    ppermute x6, waiting for transfers between devices, swap(): return (lax.ppermute(one, axis, near), lax.ppermute(two, axis, far))  4.46 us
  transfers between devices with their start and end apart: 17, of which 10 were waited for; matrix products, arithmetic and copies ran while one was open for 0% of the time, Pallas kernels for 0%

commit v1 on v0

--- a/solution.py
+++ b/solution.py
@@ -71,12 +71,10 @@
             pltpu.make_async_copy(mask_in, mask, sems.at[1]),
             pltpu.make_async_copy(ids_in, ids, sems.at[2]),
         ]
-        for item in small:
-            item.start()
         for x in range(slots):
             copy(x).start()
         for item in small:
-            item.wait()
+            item.start()
         lane = lax.broadcasted_iota(jnp.int32, (columns, LANES), 1)
         one = lax.broadcasted_iota(jnp.int32, (1, LANES), 1)
         z_up = jnp.where(one == LANES - 1, 0.0, 1.0 + advection[2])
@@ -131,6 +129,9 @@
                 acc[...] = gram
             else:
                 acc[...] += gram
+            if x == 0:
+                for item in small:
+                    item.wait()
             if x > 0:
                 first, last = apply(x - 1, first, last)
         first, last = apply(sx - 1, first, last)
@@ -186,7 +187,7 @@
     rows = rows2 // 2
     columns = applied.shape[0]
     half = rows // 2
-    size = rows + half + columns + 16
+    size = rows + half + columns // 2 + 16
     chunks = 4
 
     def kernel(halves, applied, own, xa, xb, ya, yb, za, zb, both, keep, give, passed, packed):
@@ -228,12 +229,12 @@
                 both[columns:, cols] = rest
             if (x + 1) % (sx // chunks) == 0:
                 cols = slice((x + 1 - sx // chunks) * sy * LANES, (x + 1) * sy * LANES)
-                one = narrow(halves[:, cols], both[:, cols], ROW_DIMS)
+                one = narrow(both[:, cols], halves[:, cols], ROW_DIMS)
                 two = narrow(both[:, cols], both[:, cols], ROW_DIMS)
                 cross = one if cross is None else cross + one
                 square = two if square is None else square + two
-        mixed = cross[0:rows, :] + cross[rows:, :]
-        coeffs = (mixed[:, 0:columns] + mixed[:, columns:]) * scale
+        mixed = cross[:, 0:rows] + cross[:, rows:]
+        turned = (mixed[0:columns, :] + mixed[columns:, :]) * scale
         square = square[0:columns, :] + square[columns:, :]
         square = (square[:, 0:columns] + square[:, columns:]) * scale
         corner = own[half:, half:] * scale
@@ -241,12 +242,13 @@
         col = lax.broadcasted_iota(jnp.int32, (half, half), 1)
         packed[0:half, :] = own[0:half, half:] * scale
         packed[half:rows, :] = jnp.where(row <= col, own[0:half, 0:half] * scale, corner)
-        packed[rows : rows + half, 0:columns] = coeffs[0:half, :]
-        packed[rows : rows + half, columns:] = coeffs[half:, :]
-        packed[rows + half : rows + half + columns, :] = jnp.zeros((columns, LANES), F32)
-        packed[rows + half : rows + half + columns, 0:columns] = square
+        packed[rows : rows + columns, :] = turned[:, 0:half]
+        packed[rows + columns : rows + half, :] = turned[:, half:]
+        tail = rows + half + columns // 2
+        packed[rows + half : tail, 0:columns] = square[0 : columns // 2, :]
+        packed[rows + half : tail, columns:] = square[columns // 2 :, :]
         diag = jnp.sum(jnp.where(row == col, corner, 0.0), axis=0, keepdims=True)
-        packed[rows + half + columns :, :] = jnp.broadcast_to(diag, (16, LANES))
+        packed[tail:, :] = jnp.broadcast_to(diag, (16, LANES))
         core = lax.axis_index("gz") % 2
         part = size // 2
         keep[...] = packed[pl.ds(pl.multiple_of(core * part, 8), part), :]
@@ -287,18 +289,16 @@
         upper = jnp.where(row < col, mixed, 0.0)
         s11 = upper + upper.T + jnp.where(row == col, mixed, 0.0)
         lower = jnp.where(row > col, mixed, 0.0)
-        diag = packed[rows + half + columns : rows + half + columns + 1, :]
+        tail = rows + half + columns // 2
+        diag = packed[tail : tail + 1, :]
         s22 = lower + lower.T + jnp.where(row == col, diag, 0.0)
         s12 = packed[0:half, :]
-        coeffs = jnp.concatenate(
-            [packed[rows : rows + half, 0:columns], packed[rows : rows + half, columns:]], axis=0
-        )
-        coeffs_out[...] = coeffs
-        turned = coeffs.T
-        left, right = turned[:, 0:half], turned[:, half:]
+        left, right = packed[rows : rows + columns, :], packed[rows + columns : rows + half, :]
+        turned = jnp.concatenate([left, right], axis=1)
+        coeffs_out[...] = turned.T
         first = exact(left, s11) + exact(right, s12, ROW_DIMS) - 2.0 * left
         second = exact(left, s12) + exact(right, s22) - 2.0 * right
-        gram = packed[rows + half : rows + half + columns, 0:columns]
+        gram = jnp.concatenate([packed[rows + half : tail, 0:columns], packed[rows + half : tail, columns:]], axis=0)
         gram = gram + exact(first, left, ROW_DIMS) + exact(second, right, ROW_DIMS)
         gram = 0.5 * (gram + gram.T)
         eye = (

time: 83.2 us -> 82.1 us (0.987)
  waiting for transfers between devices: 22.4 us -> 21.5 us
    ppermute x11, waiting for transfers between devices: 17.9 us -> 17 us  [exchange(): return lax.ppermute(value, axis, pairs)]
where the time goes in v1:
time: 82.1 us; the launch traced here: 81 us
  Pallas kernels  33.6 us (41%)
  starting transfers between devices  24.9 us (30%)
  waiting for transfers between devices  21.5 us (26%)
  between operations  0.88 us (1%)
    ppermute x11, waiting for transfers between devices, exchange(): return lax.ppermute(value, axis, pairs)  17 us
    pallas_call x1, Pallas kernels, local_part(): pl.pallas_call(kernel, in_specs=[pl.BlockSpec(memory_space=pltpu.HBM)] *...  15.1 us
    ppermute x11, starting transfers between devices, exchange(): return lax.ppermute(value, axis, pairs)  12.9 us
    pallas_call x1, Pallas kernels, finish(): pl.pallas_call(kernel, in_specs=[vmem] * 4, out_specs=[anywhere, vmem, vm...  12.3 us
    ppermute x6, starting transfers between devices, swap(): return (lax.ppermute(one, axis, near), lax.ppermute(two, axis, far))  12.1 us
    pallas_call x1, Pallas kernels, products(): pl.pallas_call(kernel, in_specs=[vmem] * 9, out_specs=[vmem] * 4, out_sha...  6.18 us
    ppermute x6, waiting for transfers between devices, swap(): return (lax.ppermute(one, axis, near), lax.ppermute(two, axis, far))  4.46 us
  transfers between devices with their start and end apart: 17, of which 10 were waited for; matrix products, arithmetic and copies ran while one was open for 0% of the time, Pallas kernels for 0%

profile of v1, /device:TPU:0, one launch (start us, length us, event | category | flops | bytes accessed | tf_op | source)
XLA Modules:
  0.0 81.0 jit_solution(8699489324790116303)
XLA Ops:
  0.6 15.1 %local_part.1 = (bf16[512,16384]{1,0:T(8,128)(2,1)S(1)}, f32[64,16384]{1,0:T(8,128)S(1)}, f32[256,256]{1,0:T(8,128)S(1)}, f32[16,64,128]{2,1,0:T(8,128)S(1)}, f3...) custom-call(f32[64]{0:T(128)} %table_in.1, ...), custom_call_target="tpu_custom_call" | custom-call | tf_op jit(solution)/shard_map/local_part/pallas_call | solution.py:155
  15.8 2.9 %collective-permute-start.1 = (f32[16,64,128]{2,1,0:T(8,128)S(1)}, f32[16,64,128]{2,1,0:T(8,128)S(1)}, u32[]{:S(2)}, u32[]{:S(2)}) collective-permute-start(f32[16,64,128]{2,1,0:T(8,128)S(1)} %get-tuple-element.23), channel_id=1, source_target_pairs={{0,7},{1,2},{2,1},{3,4},{4,3},{5,6},{6,5},{7,0},{8,15},{9,10},{10,... | collective-permute-start | bytes 1572872 | tf_op jit(solution)/shard_map/ppermute | solution.py:380
  18.7 1.9 %collective-permute-start.2 = (f32[8,64,128]{2,1,0:T(8,128)S(1)}, f32[8,64,128]{2,1,0:T(8,128)S(1)}, u32[]{:S(2)}, u32[]{:S(2)}) collective-permute-start(f32[8,64,128]{2,1,0:T(8,128)S(1)} %get-tuple-element.24), channel_id=1, source_target_pairs={{0,32},{32,0},{64,96},{96,64},{1,33},{33,1},{65,97},{97,65},{2,34}... | collective-permute-start | bytes 786440 | tf_op jit(solution)/shard_map/ppermute | solution.py:380
  20.6 2.5 %collective-permute-start.3 = (f32[8,64,128]{2,1,0:T(8,128)S(1)}, f32[8,64,128]{2,1,0:T(8,128)S(1)}, u32[]{:S(2)}, u32[]{:S(2)}) collective-permute-start(f32[8,64,128]{2,1,0:T(8,128)S(1)} %get-tuple-element.25), channel_id=1, source_target_pairs={{0,96},{32,64},{64,32},{96,0},{1,97},{33,65},{65,33},{97,1},{2,98}... | collective-permute-start | bytes 786440 | tf_op jit(solution)/shard_map/ppermute | solution.py:380
  23.2 1.6 %collective-permute-start.4 = (f32[64,128]{1,0:T(8,128)S(1)}, f32[64,128]{1,0:T(8,128)S(1)}, u32[]{:S(2)}, u32[]{:S(2)}) collective-permute-start(f32[64,128]{1,0:T(8,128)S(1)} %get-tuple-element.26), channel_id=1, source_target_pairs={{0,8},{8,0},{16,24},{24,16},{1,9},{9,1},{17,25},{25,17},{2,10},{10... | collective-permute-start | bytes 98312 | tf_op jit(solution)/shard_map/ppermute | solution.py:380
  24.7 2.3 %collective-permute-done.4.za = f32[64,128]{1,0:T(8,128)S(1)} collective-permute-done((f32[64,128]{1,0:T(8,128)S(1)}, f32[64,128]{1,0:T(8,128)S(1)}, u32[]{:S(2)}, u32[]{:S(2)}) %collective-permute-start.4) | collective-permute-done | bytes 32800 | tf_op jit(solution)/shard_map/ppermute | solution.py:380
  27.1 3.0 %collective-permute-start.5 = (f32[64,128]{1,0:T(8,128)S(1)}, f32[64,128]{1,0:T(8,128)S(1)}, u32[]{:S(2)}, u32[]{:S(2)}) collective-permute-start(f32[64,128]{1,0:T(8,128)S(1)} %get-tuple-element.27), channel_id=1, source_target_pairs={{0,24},{8,16},{16,8},{24,0},{1,25},{9,17},{17,9},{25,1},{2,26},{10... | collective-permute-start | bytes 98312 | tf_op jit(solution)/shard_map/ppermute | solution.py:380
  30.1 2.1 %collective-permute-done.5.zb = f32[64,128]{1,0:T(8,128)S(1)} collective-permute-done((f32[64,128]{1,0:T(8,128)S(1)}, f32[64,128]{1,0:T(8,128)S(1)}, u32[]{:S(2)}, u32[]{:S(2)}) %collective-permute-start.5) | collective-permute-done | bytes 32800 | tf_op jit(solution)/shard_map/ppermute | solution.py:380
  32.2 6.2 %products.1 = (bf16[128,16384]{1,0:T(8,128)(2,1)S(1)}, f32[216,128]{1,0:T(8,128)S(1)}, f32[216,128]{1,0:T(8,128)S(1)}, bf16[512,16384]{1,0:T(8,128)(2,1)S(1)}) custom-call(bf16[512,16384]{1,0:T(8,128)(2,1)S(1)} %get-tuple-element.19.halves, f32[64,16384]{1,0:T(8,128)S(1)} %get-tuple-element.20.applied, ...), custom_call_target="tpu_custom_call", output_to_operand_aliasing={{3}: (0, {})} | custom-call | tf_op jit(solution)/shard_map/products/pallas_call | solution.py:258
  38.5 1.3 %collective-permute-done.6 = f32[216,128]{1,0:T(8,128)S(1)} collective-permute-done((f32[216,128]{1,0:T(8,128)S(1)}, f32[216,128]{1,0:T(8,128)S(1)}, u32[]{:S(2)}, u32[]{:S(2)}) %collective-permute-start.6) | collective-permute-done | bytes 110624 | tf_op jit(solution)/shard_map/ppermute | solution.py:18
  39.8 0.9 %collective-permute-start.9 = (f32[216,128]{1,0:T(8,128)S(1)}, f32[216,128]{1,0:T(8,128)S(1)}, u32[]{:S(2)}, u32[]{:S(2)}) collective-permute-start(f32[216,128]{1,0:T(8,128)S(1)} %add.30), channel_id=1, source_target_pairs={{0,6},{1,7},{2,4},{3,5},{4,2},{5,3},{6,0},{7,1},{8,14},{9,15},{10,... | collective-permute-start | bytes 331784 | tf_op jit(solution)/shard_map/ppermute | solution.py:18
  41.2 2.7 %collective-permute-start.7 = (f32[216,128]{1,0:T(8,128)S(1)}, f32[216,128]{1,0:T(8,128)S(1)}, u32[]{:S(2)}, u32[]{:S(2)}) collective-permute-start(f32[216,128]{1,0:T(8,128)S(1)} %add.30), channel_id=1, source_target_pairs={{0,2},{1,3},{2,0},{3,1},{4,6},{5,7},{6,4},{7,5},{8,10},{9,11},{10,... | collective-permute-start | bytes 331784 | tf_op jit(solution)/shard_map/ppermute | solution.py:18
  44.0 4.6 %collective-permute-done.9 = f32[216,128]{1,0:T(8,128)S(1)} collective-permute-done((f32[216,128]{1,0:T(8,128)S(1)}, f32[216,128]{1,0:T(8,128)S(1)}, u32[]{:S(2)}, u32[]{:S(2)}) %collective-permute-start.9) | collective-permute-done | bytes 110624 | tf_op jit(solution)/shard_map/ppermute | solution.py:18
  49.2 3.1 %collective-permute-start.12 = (f32[216,128]{1,0:T(8,128)S(1)}, f32[216,128]{1,0:T(8,128)S(1)}, u32[]{:S(2)}, u32[]{:S(2)}) collective-permute-start(f32[216,128]{1,0:T(8,128)S(1)} %add_add_fusion.2), channel_id=1, source_target_pairs={{0,24},{8,16},{16,8},{24,0},{1,25},{9,17},{17,9},{25,1},{2,26},{10... | collective-permute-start | bytes 331784 | tf_op jit(solution)/shard_map/ppermute | solution.py:18
  52.3 1.1 %collective-permute-start.10 = (f32[216,128]{1,0:T(8,128)S(1)}, f32[216,128]{1,0:T(8,128)S(1)}, u32[]{:S(2)}, u32[]{:S(2)}) collective-permute-start(f32[216,128]{1,0:T(8,128)S(1)} %add_add_fusion.2), channel_id=1, source_target_pairs={{0,8},{8,0},{16,24},{24,16},{1,9},{9,1},{17,25},{25,17},{2,10},{10... | collective-permute-start | bytes 331784 | tf_op jit(solution)/shard_map/ppermute | solution.py:18
  53.3 3.0 %collective-permute-done.12 = f32[216,128]{1,0:T(8,128)S(1)} collective-permute-done((f32[216,128]{1,0:T(8,128)S(1)}, f32[216,128]{1,0:T(8,128)S(1)}, u32[]{:S(2)}, u32[]{:S(2)}) %collective-permute-start.12) | collective-permute-done | bytes 110624 | tf_op jit(solution)/shard_map/ppermute | solution.py:18
  56.4 2.3 %collective-permute-done.11 = f32[216,128]{1,0:T(8,128)S(1)} collective-permute-done((f32[216,128]{1,0:T(8,128)S(1)}, f32[216,128]{1,0:T(8,128)S(1)}, u32[]{:S(2)}, u32[]{:S(2)}) %collective-permute-start.11) | collective-permute-done | bytes 110624 | tf_op jit(solution)/shard_map/ppermute | solution.py:18
  58.7 0.8 collective-permute-start.15
  59.5 2.4 %collective-permute-start.14 = (f32[216,128]{1,0:T(8,128)S(1)}, f32[216,128]{1,0:T(8,128)S(1)}, u32[]{:S(2)}, u32[]{:S(2)}) collective-permute-start(f32[216,128]{1,0:T(8,128)S(1)} %add_add_fusion.1), channel_id=1, source_target_pairs={{0,64},{32,96},{64,0},{96,32},{1,65},{33,97},{65,1},{97,33},{2,66}... | collective-permute-start | bytes 331784 | tf_op jit(solution)/shard_map/ppermute | solution.py:18
  61.9 1.0 %collective-permute-start.13 = (f32[216,128]{1,0:T(8,128)S(1)}, f32[216,128]{1,0:T(8,128)S(1)}, u32[]{:S(2)}, u32[]{:S(2)}) collective-permute-start(f32[216,128]{1,0:T(8,128)S(1)} %add_add_fusion.1), channel_id=1, source_target_pairs={{0,32},{32,0},{64,96},{96,64},{1,33},{33,1},{65,97},{97,65},{2,34}... | collective-permute-start | bytes 331784 | tf_op jit(solution)/shard_map/ppermute | solution.py:18
  62.9 3.0 %collective-permute-done.15 = f32[216,128]{1,0:T(8,128)S(1)} collective-permute-done((f32[216,128]{1,0:T(8,128)S(1)}, f32[216,128]{1,0:T(8,128)S(1)}, u32[]{:S(2)}, u32[]{:S(2)}) %collective-permute-start.15) | collective-permute-done | bytes 110624 | tf_op jit(solution)/shard_map/ppermute | solution.py:18
  65.9 0.9 %collective-permute-done.13 = f32[216,128]{1,0:T(8,128)S(1)} collective-permute-done((f32[216,128]{1,0:T(8,128)S(1)}, f32[216,128]{1,0:T(8,128)S(1)}, u32[]{:S(2)}, u32[]{:S(2)}) %collective-permute-start.13) | collective-permute-done | bytes 110624 | tf_op jit(solution)/shard_map/ppermute | solution.py:18
  67.1 1.3 %collective-permute-done.16.other = f32[216,128]{1,0:T(8,128)S(1)} collective-permute-done((f32[216,128]{1,0:T(8,128)S(1)}, f32[216,128]{1,0:T(8,128)S(1)}, u32[]{:S(2)}, u32[]{:S(2)}) %collective-permute-start.16) | collective-permute-done | bytes 110624 | tf_op jit(solution)/shard_map/ppermute | solution.py:18
  68.5 12.3 %finish.1 = (f32[64,8,16,128]{3,2,1,0:T(8,128)}, f32[256,64]{1,0:T(8,128)}, f32[64,64]{1,0:T(8,128)}) custom-call(f32[216,128]{1,0:T(8,128)S(1)} %add_add_fusion.part, f32[216,128]{1,0:T(8,128)S(1)} %collective-permute-done.16.other, bf16[512,16384]{1,0:T(8,128)(2,1)S(1)} %get-tuple-element.30.basis, bf16[128,16384]{1,0:T(8,128)(2,1)S(1)} %get-tuple-element.31.block), custom_call_target="tpu_custom_call" | custom-call | tf_op jit(solution)/shard_map/finish/pallas_call | solution.py:356
  (17 shorter events, 1.7 us)
Async XLA Ops:
  15.7 16.5 %collective-permute-start = (f32[16,64,128]{2,1,0:T(8,128)S(1)}, f32[16,64,128]{2,1,0:T(8,128)S(1)}, u32[]{:S(2)}, u32[]{:S(2)}) collective-permute-start(f32[16,64,128]{2,1,0:T(8,128)S(1)} %get-tuple-element.22), channel_id=1, source_target_pairs={{0,1},{1,0},{2,3},{3,2},{4,5},{5,4},{6,7},{7,6},{8,9},{9,8},{10,11... | collective-permute-start | bytes 1572872 | tf_op jit(solution)/shard_map/ppermute | solution.py:380
  15.8 16.4 %collective-permute-start.1 = (f32[16,64,128]{2,1,0:T(8,128)S(1)}, f32[16,64,128]{2,1,0:T(8,128)S(1)}, u32[]{:S(2)}, u32[]{:S(2)}) collective-permute-start(f32[16,64,128]{2,1,0:T(8,128)S(1)} %get-tuple-element.23), channel_id=1, source_target_pairs={{0,7},{1,2},{2,1},{3,4},{4,3},{5,6},{6,5},{7,0},{8,15},{9,10},{10,... | collective-permute-start | bytes 1572872 | tf_op jit(solution)/shard_map/ppermute | solution.py:380
  18.7 13.5 %collective-permute-start.2 = (f32[8,64,128]{2,1,0:T(8,128)S(1)}, f32[8,64,128]{2,1,0:T(8,128)S(1)}, u32[]{:S(2)}, u32[]{:S(2)}) collective-permute-start(f32[8,64,128]{2,1,0:T(8,128)S(1)} %get-tuple-element.24), channel_id=1, source_target_pairs={{0,32},{32,0},{64,96},{96,64},{1,33},{33,1},{65,97},{97,65},{2,34}... | collective-permute-start | bytes 786440 | tf_op jit(solution)/shard_map/ppermute | solution.py:380
  20.6 11.6 %collective-permute-start.3 = (f32[8,64,128]{2,1,0:T(8,128)S(1)}, f32[8,64,128]{2,1,0:T(8,128)S(1)}, u32[]{:S(2)}, u32[]{:S(2)}) collective-permute-start(f32[8,64,128]{2,1,0:T(8,128)S(1)} %get-tuple-element.25), channel_id=1, source_target_pairs={{0,96},{32,64},{64,32},{96,0},{1,97},{33,65},{65,33},{97,1},{2,98}... | collective-permute-start | bytes 786440 | tf_op jit(solution)/shard_map/ppermute | solution.py:380
  23.2 3.9 %collective-permute-start.4 = (f32[64,128]{1,0:T(8,128)S(1)}, f32[64,128]{1,0:T(8,128)S(1)}, u32[]{:S(2)}, u32[]{:S(2)}) collective-permute-start(f32[64,128]{1,0:T(8,128)S(1)} %get-tuple-element.26), channel_id=1, source_target_pairs={{0,8},{8,0},{16,24},{24,16},{1,9},{9,1},{17,25},{25,17},{2,10},{10... | collective-permute-start | bytes 98312 | tf_op jit(solution)/shard_map/ppermute | solution.py:380
  27.1 5.1 %collective-permute-start.5 = (f32[64,128]{1,0:T(8,128)S(1)}, f32[64,128]{1,0:T(8,128)S(1)}, u32[]{:S(2)}, u32[]{:S(2)}) collective-permute-start(f32[64,128]{1,0:T(8,128)S(1)} %get-tuple-element.27), channel_id=1, source_target_pairs={{0,24},{8,16},{16,8},{24,0},{1,25},{9,17},{17,9},{25,1},{2,26},{10... | collective-permute-start | bytes 98312 | tf_op jit(solution)/shard_map/ppermute | solution.py:380
  38.4 1.3 %collective-permute-start.6 = (f32[216,128]{1,0:T(8,128)S(1)}, f32[216,128]{1,0:T(8,128)S(1)}, u32[]{:S(2)}, u32[]{:S(2)}) collective-permute-start(f32[216,128]{1,0:T(8,128)S(1)} %get-tuple-element.29), channel_id=1, source_target_pairs={{0,1},{1,0},{2,3},{3,2},{4,5},{5,4},{6,7},{7,6},{8,9},{9,8},{10,11... | collective-permute-start | bytes 331784 | tf_op jit(solution)/shard_map/ppermute | solution.py:18
  39.8 8.8 %collective-permute-start.9 = (f32[216,128]{1,0:T(8,128)S(1)}, f32[216,128]{1,0:T(8,128)S(1)}, u32[]{:S(2)}, u32[]{:S(2)}) collective-permute-start(f32[216,128]{1,0:T(8,128)S(1)} %add.30), channel_id=1, source_target_pairs={{0,6},{1,7},{2,4},{3,5},{4,2},{5,3},{6,0},{7,1},{8,14},{9,15},{10,... | collective-permute-start | bytes 331784 | tf_op jit(solution)/shard_map/ppermute | solution.py:18
  40.7 7.9 %collective-permute-start.8 = (f32[216,128]{1,0:T(8,128)S(1)}, f32[216,128]{1,0:T(8,128)S(1)}, u32[]{:S(2)}, u32[]{:S(2)}) collective-permute-start(f32[216,128]{1,0:T(8,128)S(1)} %add.30), channel_id=1, source_target_pairs={{0,4},{1,5},{2,6},{3,7},{4,0},{5,1},{6,2},{7,3},{8,12},{9,13},{10,... | collective-permute-start | bytes 331784 | tf_op jit(solution)/shard_map/ppermute | solution.py:18
  41.2 7.9 %collective-permute-start.7 = (f32[216,128]{1,0:T(8,128)S(1)}, f32[216,128]{1,0:T(8,128)S(1)}, u32[]{:S(2)}, u32[]{:S(2)}) collective-permute-start(f32[216,128]{1,0:T(8,128)S(1)} %add.30), channel_id=1, source_target_pairs={{0,2},{1,3},{2,0},{3,1},{4,6},{5,7},{6,4},{7,5},{8,10},{9,11},{10,... | collective-permute-start | bytes 331784 | tf_op jit(solution)/shard_map/ppermute | solution.py:18
  49.2 7.2 %collective-permute-start.12 = (f32[216,128]{1,0:T(8,128)S(1)}, f32[216,128]{1,0:T(8,128)S(1)}, u32[]{:S(2)}, u32[]{:S(2)}) collective-permute-start(f32[216,128]{1,0:T(8,128)S(1)} %add_add_fusion.2), channel_id=1, source_target_pairs={{0,24},{8,16},{16,8},{24,0},{1,25},{9,17},{17,9},{25,1},{2,26},{10... | collective-permute-start | bytes 331784 | tf_op jit(solution)/shard_map/ppermute | solution.py:18
  52.3 6.4 %collective-permute-start.11 = (f32[216,128]{1,0:T(8,128)S(1)}, f32[216,128]{1,0:T(8,128)S(1)}, u32[]{:S(2)}, u32[]{:S(2)}) collective-permute-start(f32[216,128]{1,0:T(8,128)S(1)} %add_add_fusion.2), channel_id=1, source_target_pairs={{0,16},{8,24},{16,0},{24,8},{1,17},{9,25},{17,1},{25,9},{2,18},{10... | collective-permute-start | bytes 331784 | tf_op jit(solution)/shard_map/ppermute | solution.py:18
  52.3 6.4 %collective-permute-start.10 = (f32[216,128]{1,0:T(8,128)S(1)}, f32[216,128]{1,0:T(8,128)S(1)}, u32[]{:S(2)}, u32[]{:S(2)}) collective-permute-start(f32[216,128]{1,0:T(8,128)S(1)} %add_add_fusion.2), channel_id=1, source_target_pairs={{0,8},{8,0},{16,24},{24,16},{1,9},{9,1},{17,25},{25,17},{2,10},{10... | collective-permute-start | bytes 331784 | tf_op jit(solution)/shard_map/ppermute | solution.py:18
  58.7 7.2 %collective-permute-start.15 = (f32[216,128]{1,0:T(8,128)S(1)}, f32[216,128]{1,0:T(8,128)S(1)}, u32[]{:S(2)}, u32[]{:S(2)}) collective-permute-start(f32[216,128]{1,0:T(8,128)S(1)} %add_add_fusion.1), channel_id=1, source_target_pairs={{0,96},{32,64},{64,32},{96,0},{1,97},{33,65},{65,33},{97,1},{2,98}... | collective-permute-start | bytes 331784 | tf_op jit(solution)/shard_map/ppermute | solution.py:18
  59.5 6.4 %collective-permute-start.14 = (f32[216,128]{1,0:T(8,128)S(1)}, f32[216,128]{1,0:T(8,128)S(1)}, u32[]{:S(2)}, u32[]{:S(2)}) collective-permute-start(f32[216,128]{1,0:T(8,128)S(1)} %add_add_fusion.1), channel_id=1, source_target_pairs={{0,64},{32,96},{64,0},{96,32},{1,65},{33,97},{65,1},{97,33},{2,66}... | collective-permute-start | bytes 331784 | tf_op jit(solution)/shard_map/ppermute | solution.py:18
  61.9 4.9 %collective-permute-start.13 = (f32[216,128]{1,0:T(8,128)S(1)}, f32[216,128]{1,0:T(8,128)S(1)}, u32[]{:S(2)}, u32[]{:S(2)}) collective-permute-start(f32[216,128]{1,0:T(8,128)S(1)} %add_add_fusion.1), channel_id=1, source_target_pairs={{0,32},{32,0},{64,96},{96,64},{1,33},{33,1},{65,97},{97,65},{2,34}... | collective-permute-start | bytes 331784 | tf_op jit(solution)/shard_map/ppermute | solution.py:18
  66.8 1.6 %collective-permute-start.16 = (f32[216,128]{1,0:T(8,128)S(1)}, f32[216,128]{1,0:T(8,128)S(1)}, u32[]{:S(2)}, u32[]{:S(2)}) collective-permute-start(f32[216,128]{1,0:T(8,128)S(1)} %add_add_fusion.part), channel_id=1, source_target_pairs={{0,1},{1,0},{2,3},{3,2},{4,5},{5,4},{6,7},{7,6},{8,9},{9,8},{10,11... | collective-permute-start | bytes 331784 | tf_op jit(solution)/shard_map/ppermute | solution.py:18

commit v2 on v1

--- a/solution.py
+++ b/solution.py
@@ -278,6 +278,7 @@
     half = rows // 2
     width = sy * LANES
     size = part.shape[0]
+    depth = 4
 
     def kernel(part, other, basis, block, fresh, coeffs_out, factor_out, staged, packed, residual, sem_out):
         core = lax.axis_index("gz") % 2
@@ -296,10 +297,12 @@
         left, right = packed[rows : rows + columns, :], packed[rows + columns : rows + half, :]
         turned = jnp.concatenate([left, right], axis=1)
         coeffs_out[...] = turned.T
-        first = exact(left, s11) + exact(right, s12, ROW_DIMS) - 2.0 * left
-        second = exact(left, s12) + exact(right, s22) - 2.0 * right
+        square = jnp.concatenate(
+            [jnp.concatenate([s11, s12], axis=1), jnp.concatenate([s12.T, s22], axis=1)], axis=0
+        )
+        middle = exact(turned, square) - 2.0 * turned
         gram = jnp.concatenate([packed[rows + half : tail, 0:columns], packed[rows + half : tail, columns:]], axis=0)
-        gram = gram + exact(first, left, ROW_DIMS) + exact(second, right, ROW_DIMS)
+        gram = gram + exact(middle, turned, ROW_DIMS)
         gram = 0.5 * (gram + gram.T)
         eye = (
             lax.broadcasted_iota(jnp.int32, (columns, columns), 0)
@@ -340,16 +343,16 @@
             cols = slice(x * width, (x + 1) * width)
             big = narrow(inv_both, residual[0:columns, cols])
             value = big[0:columns] + big[columns:] + narrow(inv_both[0:columns], residual[columns:, cols])
-            slot = x % 2
-            if x >= 2:
-                outs[x - 2].wait()
+            slot = x % depth
+            if x >= depth:
+                outs[x - depth].wait()
             for group in range(0, sy, 8):
                 rows_y = [value[:, (group + y) * LANES : (group + y + 1) * LANES][None] for y in range(8)]
                 staged[slot, :, group : group + 8, :] = pltpu.einshape("yjl->jyl", jnp.concatenate(rows_y, axis=0))
             outs.append(pltpu.make_async_copy(staged.at[slot], fresh.at[:, x], sem_out.at[slot]))
             outs[x].start()
-        outs[sx - 2].wait()
-        outs[sx - 1].wait()
+        for x in range(sx - depth, sx):
+            outs[x].wait()
 
     vmem = pl.BlockSpec(memory_space=pltpu.VMEM)
     anywhere = pl.BlockSpec(memory_space=pl.ANY)
@@ -363,10 +366,10 @@
             jax.ShapeDtypeStruct((columns, columns), F32),
         ],
         scratch_shapes=[
-            pltpu.VMEM((2, columns, sy, LANES), F32),
+            pltpu.VMEM((depth, columns, sy, LANES), F32),
             pltpu.VMEM((2 * size, LANES), F32),
             pltpu.VMEM(applied.shape, BF16),
-            pltpu.SemaphoreType.DMA((2,)),
+            pltpu.SemaphoreType.DMA((depth,)),
         ],
         compiler_params=pltpu.CompilerParams(vmem_limit_bytes=14 * 2**20),
         name="finish",

time: 82.1 us -> 80.5 us (0.981)
  Pallas kernels: 33.6 us -> 31.9 us
    pallas_call x1, Pallas kernels: 12.3 us -> 10.7 us  [finish(): pl.pallas_call(kernel, in_specs=[vmem] * 4, out_specs=[anywhere, vmem, vm...]
where the time goes in v2:
time: 80.5 us; the launch traced here: 79.3 us
  Pallas kernels  31.9 us (40%)
  starting transfers between devices  24.9 us (31%)
  waiting for transfers between devices  21.5 us (27%)
  between operations  0.88 us (1%)
    ppermute x11, waiting for transfers between devices, exchange(): return lax.ppermute(value, axis, pairs)  17 us
    pallas_call x1, Pallas kernels, local_part(): pl.pallas_call(kernel, in_specs=[pl.BlockSpec(memory_space=pltpu.HBM)] *...  15.1 us
    ppermute x11, starting transfers between devices, exchange(): return lax.ppermute(value, axis, pairs)  12.9 us
    ppermute x6, starting transfers between devices, swap(): return (lax.ppermute(one, axis, near), lax.ppermute(two, axis, far))  12.1 us
    pallas_call x1, Pallas kernels, finish(): pl.pallas_call(kernel, in_specs=[vmem] * 4, out_specs=[anywhere, vmem, vm...  10.7 us
    pallas_call x1, Pallas kernels, products(): pl.pallas_call(kernel, in_specs=[vmem] * 9, out_specs=[vmem] * 4, out_sha...  6.18 us
    ppermute x6, waiting for transfers between devices, swap(): return (lax.ppermute(one, axis, near), lax.ppermute(two, axis, far))  4.46 us
  transfers between devices with their start and end apart: 17, of which 10 were waited for; matrix products, arithmetic and copies ran while one was open for 0% of the time, Pallas kernels for 0%

profile of v2, /device:TPU:0, one launch (start us, length us, event | category | flops | bytes accessed | tf_op | source)
XLA Modules:
  0.0 79.3 jit_solution(726193993794933556)
XLA Ops:
  0.6 15.1 %local_part.1 = (bf16[512,16384]{1,0:T(8,128)(2,1)S(1)}, f32[64,16384]{1,0:T(8,128)S(1)}, f32[256,256]{1,0:T(8,128)S(1)}, f32[16,64,128]{2,1,0:T(8,128)S(1)}, f3...) custom-call(f32[64]{0:T(128)} %table_in.1, ...), custom_call_target="tpu_custom_call" | custom-call | tf_op jit(solution)/shard_map/local_part/pallas_call | solution.py:155
  15.8 2.9 %collective-permute-start.1 = (f32[16,64,128]{2,1,0:T(8,128)S(1)}, f32[16,64,128]{2,1,0:T(8,128)S(1)}, u32[]{:S(2)}, u32[]{:S(2)}) collective-permute-start(f32[16,64,128]{2,1,0:T(8,128)S(1)} %get-tuple-element.23), channel_id=1, source_target_pairs={{0,7},{1,2},{2,1},{3,4},{4,3},{5,6},{6,5},{7,0},{8,15},{9,10},{10,... | collective-permute-start | bytes 1572872 | tf_op jit(solution)/shard_map/ppermute | solution.py:383
  18.7 1.9 %collective-permute-start.2 = (f32[8,64,128]{2,1,0:T(8,128)S(1)}, f32[8,64,128]{2,1,0:T(8,128)S(1)}, u32[]{:S(2)}, u32[]{:S(2)}) collective-permute-start(f32[8,64,128]{2,1,0:T(8,128)S(1)} %get-tuple-element.24), channel_id=1, source_target_pairs={{0,32},{32,0},{64,96},{96,64},{1,33},{33,1},{65,97},{97,65},{2,34}... | collective-permute-start | bytes 786440 | tf_op jit(solution)/shard_map/ppermute | solution.py:383
  20.6 2.5 %collective-permute-start.3 = (f32[8,64,128]{2,1,0:T(8,128)S(1)}, f32[8,64,128]{2,1,0:T(8,128)S(1)}, u32[]{:S(2)}, u32[]{:S(2)}) collective-permute-start(f32[8,64,128]{2,1,0:T(8,128)S(1)} %get-tuple-element.25), channel_id=1, source_target_pairs={{0,96},{32,64},{64,32},{96,0},{1,97},{33,65},{65,33},{97,1},{2,98}... | collective-permute-start | bytes 786440 | tf_op jit(solution)/shard_map/ppermute | solution.py:383
  23.2 1.6 %collective-permute-start.4 = (f32[64,128]{1,0:T(8,128)S(1)}, f32[64,128]{1,0:T(8,128)S(1)}, u32[]{:S(2)}, u32[]{:S(2)}) collective-permute-start(f32[64,128]{1,0:T(8,128)S(1)} %get-tuple-element.26), channel_id=1, source_target_pairs={{0,8},{8,0},{16,24},{24,16},{1,9},{9,1},{17,25},{25,17},{2,10},{10... | collective-permute-start | bytes 98312 | tf_op jit(solution)/shard_map/ppermute | solution.py:383
  24.7 2.3 %collective-permute-done.4.za = f32[64,128]{1,0:T(8,128)S(1)} collective-permute-done((f32[64,128]{1,0:T(8,128)S(1)}, f32[64,128]{1,0:T(8,128)S(1)}, u32[]{:S(2)}, u32[]{:S(2)}) %collective-permute-start.4) | collective-permute-done | bytes 32800 | tf_op jit(solution)/shard_map/ppermute | solution.py:383
  27.1 3.0 %collective-permute-start.5 = (f32[64,128]{1,0:T(8,128)S(1)}, f32[64,128]{1,0:T(8,128)S(1)}, u32[]{:S(2)}, u32[]{:S(2)}) collective-permute-start(f32[64,128]{1,0:T(8,128)S(1)} %get-tuple-element.27), channel_id=1, source_target_pairs={{0,24},{8,16},{16,8},{24,0},{1,25},{9,17},{17,9},{25,1},{2,26},{10... | collective-permute-start | bytes 98312 | tf_op jit(solution)/shard_map/ppermute | solution.py:383
  30.1 2.1 %collective-permute-done.5.zb = f32[64,128]{1,0:T(8,128)S(1)} collective-permute-done((f32[64,128]{1,0:T(8,128)S(1)}, f32[64,128]{1,0:T(8,128)S(1)}, u32[]{:S(2)}, u32[]{:S(2)}) %collective-permute-start.5) | collective-permute-done | bytes 32800 | tf_op jit(solution)/shard_map/ppermute | solution.py:383
  32.2 6.2 %products.1 = (bf16[128,16384]{1,0:T(8,128)(2,1)S(1)}, f32[216,128]{1,0:T(8,128)S(1)}, f32[216,128]{1,0:T(8,128)S(1)}, bf16[512,16384]{1,0:T(8,128)(2,1)S(1)}) custom-call(bf16[512,16384]{1,0:T(8,128)(2,1)S(1)} %get-tuple-element.19.halves, f32[64,16384]{1,0:T(8,128)S(1)} %get-tuple-element.20.applied, ...), custom_call_target="tpu_custom_call", output_to_operand_aliasing={{3}: (0, {})} | custom-call | tf_op jit(solution)/shard_map/products/pallas_call | solution.py:258
  38.5 1.3 %collective-permute-done.6 = f32[216,128]{1,0:T(8,128)S(1)} collective-permute-done((f32[216,128]{1,0:T(8,128)S(1)}, f32[216,128]{1,0:T(8,128)S(1)}, u32[]{:S(2)}, u32[]{:S(2)}) %collective-permute-start.6) | collective-permute-done | bytes 110624 | tf_op jit(solution)/shard_map/ppermute | solution.py:18
  39.8 0.9 %collective-permute-start.9 = (f32[216,128]{1,0:T(8,128)S(1)}, f32[216,128]{1,0:T(8,128)S(1)}, u32[]{:S(2)}, u32[]{:S(2)}) collective-permute-start(f32[216,128]{1,0:T(8,128)S(1)} %add.30), channel_id=1, source_target_pairs={{0,6},{1,7},{2,4},{3,5},{4,2},{5,3},{6,0},{7,1},{8,14},{9,15},{10,... | collective-permute-start | bytes 331784 | tf_op jit(solution)/shard_map/ppermute | solution.py:18
  41.2 2.7 %collective-permute-start.7 = (f32[216,128]{1,0:T(8,128)S(1)}, f32[216,128]{1,0:T(8,128)S(1)}, u32[]{:S(2)}, u32[]{:S(2)}) collective-permute-start(f32[216,128]{1,0:T(8,128)S(1)} %add.30), channel_id=1, source_target_pairs={{0,2},{1,3},{2,0},{3,1},{4,6},{5,7},{6,4},{7,5},{8,10},{9,11},{10,... | collective-permute-start | bytes 331784 | tf_op jit(solution)/shard_map/ppermute | solution.py:18
  44.0 4.6 %collective-permute-done.9 = f32[216,128]{1,0:T(8,128)S(1)} collective-permute-done((f32[216,128]{1,0:T(8,128)S(1)}, f32[216,128]{1,0:T(8,128)S(1)}, u32[]{:S(2)}, u32[]{:S(2)}) %collective-permute-start.9) | collective-permute-done | bytes 110624 | tf_op jit(solution)/shard_map/ppermute | solution.py:18
  49.2 3.1 %collective-permute-start.12 = (f32[216,128]{1,0:T(8,128)S(1)}, f32[216,128]{1,0:T(8,128)S(1)}, u32[]{:S(2)}, u32[]{:S(2)}) collective-permute-start(f32[216,128]{1,0:T(8,128)S(1)} %add_add_fusion.2), channel_id=1, source_target_pairs={{0,24},{8,16},{16,8},{24,0},{1,25},{9,17},{17,9},{25,1},{2,26},{10... | collective-permute-start | bytes 331784 | tf_op jit(solution)/shard_map/ppermute | solution.py:18
  52.3 1.1 %collective-permute-start.10 = (f32[216,128]{1,0:T(8,128)S(1)}, f32[216,128]{1,0:T(8,128)S(1)}, u32[]{:S(2)}, u32[]{:S(2)}) collective-permute-start(f32[216,128]{1,0:T(8,128)S(1)} %add_add_fusion.2), channel_id=1, source_target_pairs={{0,8},{8,0},{16,24},{24,16},{1,9},{9,1},{17,25},{25,17},{2,10},{10... | collective-permute-start | bytes 331784 | tf_op jit(solution)/shard_map/ppermute | solution.py:18
  53.3 3.0 %collective-permute-done.12 = f32[216,128]{1,0:T(8,128)S(1)} collective-permute-done((f32[216,128]{1,0:T(8,128)S(1)}, f32[216,128]{1,0:T(8,128)S(1)}, u32[]{:S(2)}, u32[]{:S(2)}) %collective-permute-start.12) | collective-permute-done | bytes 110624 | tf_op jit(solution)/shard_map/ppermute | solution.py:18
  56.4 2.3 %collective-permute-done.11 = f32[216,128]{1,0:T(8,128)S(1)} collective-permute-done((f32[216,128]{1,0:T(8,128)S(1)}, f32[216,128]{1,0:T(8,128)S(1)}, u32[]{:S(2)}, u32[]{:S(2)}) %collective-permute-start.11) | collective-permute-done | bytes 110624 | tf_op jit(solution)/shard_map/ppermute | solution.py:18
  58.7 0.8 collective-permute-start.15
  59.5 2.4 %collective-permute-start.14 = (f32[216,128]{1,0:T(8,128)S(1)}, f32[216,128]{1,0:T(8,128)S(1)}, u32[]{:S(2)}, u32[]{:S(2)}) collective-permute-start(f32[216,128]{1,0:T(8,128)S(1)} %add_add_fusion.1), channel_id=1, source_target_pairs={{0,64},{32,96},{64,0},{96,32},{1,65},{33,97},{65,1},{97,33},{2,66}... | collective-permute-start | bytes 331784 | tf_op jit(solution)/shard_map/ppermute | solution.py:18
  61.9 1.0 %collective-permute-start.13 = (f32[216,128]{1,0:T(8,128)S(1)}, f32[216,128]{1,0:T(8,128)S(1)}, u32[]{:S(2)}, u32[]{:S(2)}) collective-permute-start(f32[216,128]{1,0:T(8,128)S(1)} %add_add_fusion.1), channel_id=1, source_target_pairs={{0,32},{32,0},{64,96},{96,64},{1,33},{33,1},{65,97},{97,65},{2,34}... | collective-permute-start | bytes 331784 | tf_op jit(solution)/shard_map/ppermute | solution.py:18
  62.9 3.0 %collective-permute-done.15 = f32[216,128]{1,0:T(8,128)S(1)} collective-permute-done((f32[216,128]{1,0:T(8,128)S(1)}, f32[216,128]{1,0:T(8,128)S(1)}, u32[]{:S(2)}, u32[]{:S(2)}) %collective-permute-start.15) | collective-permute-done | bytes 110624 | tf_op jit(solution)/shard_map/ppermute | solution.py:18
  65.9 0.9 %collective-permute-done.13 = f32[216,128]{1,0:T(8,128)S(1)} collective-permute-done((f32[216,128]{1,0:T(8,128)S(1)}, f32[216,128]{1,0:T(8,128)S(1)}, u32[]{:S(2)}, u32[]{:S(2)}) %collective-permute-start.13) | collective-permute-done | bytes 110624 | tf_op jit(solution)/shard_map/ppermute | solution.py:18
  67.1 1.3 %collective-permute-done.16.other = f32[216,128]{1,0:T(8,128)S(1)} collective-permute-done((f32[216,128]{1,0:T(8,128)S(1)}, f32[216,128]{1,0:T(8,128)S(1)}, u32[]{:S(2)}, u32[]{:S(2)}) %collective-permute-start.16) | collective-permute-done | bytes 110624 | tf_op jit(solution)/shard_map/ppermute | solution.py:18
  68.5 10.7 %finish.1 = (f32[64,8,16,128]{3,2,1,0:T(8,128)}, f32[256,64]{1,0:T(8,128)}, f32[64,64]{1,0:T(8,128)}) custom-call(f32[216,128]{1,0:T(8,128)S(1)} %add_add_fusion.part, f32[216,128]{1,0:T(8,128)S(1)} %collective-permute-done.16.other, bf16[512,16384]{1,0:T(8,128)(2,1)S(1)} %get-tuple-element.30.basis, bf16[128,16384]{1,0:T(8,128)(2,1)S(1)} %get-tuple-element.31.block), custom_call_target="tpu_custom_call" | custom-call | tf_op jit(solution)/shard_map/finish/pallas_call | solution.py:359
  (17 shorter events, 1.7 us)
Async XLA Ops:
  15.7 16.5 %collective-permute-start = (f32[16,64,128]{2,1,0:T(8,128)S(1)}, f32[16,64,128]{2,1,0:T(8,128)S(1)}, u32[]{:S(2)}, u32[]{:S(2)}) collective-permute-start(f32[16,64,128]{2,1,0:T(8,128)S(1)} %get-tuple-element.22), channel_id=1, source_target_pairs={{0,1},{1,0},{2,3},{3,2},{4,5},{5,4},{6,7},{7,6},{8,9},{9,8},{10,11... | collective-permute-start | bytes 1572872 | tf_op jit(solution)/shard_map/ppermute | solution.py:383
  15.8 16.4 %collective-permute-start.1 = (f32[16,64,128]{2,1,0:T(8,128)S(1)}, f32[16,64,128]{2,1,0:T(8,128)S(1)}, u32[]{:S(2)}, u32[]{:S(2)}) collective-permute-start(f32[16,64,128]{2,1,0:T(8,128)S(1)} %get-tuple-element.23), channel_id=1, source_target_pairs={{0,7},{1,2},{2,1},{3,4},{4,3},{5,6},{6,5},{7,0},{8,15},{9,10},{10,... | collective-permute-start | bytes 1572872 | tf_op jit(solution)/shard_map/ppermute | solution.py:383
  18.7 13.5 %collective-permute-start.2 = (f32[8,64,128]{2,1,0:T(8,128)S(1)}, f32[8,64,128]{2,1,0:T(8,128)S(1)}, u32[]{:S(2)}, u32[]{:S(2)}) collective-permute-start(f32[8,64,128]{2,1,0:T(8,128)S(1)} %get-tuple-element.24), channel_id=1, source_target_pairs={{0,32},{32,0},{64,96},{96,64},{1,33},{33,1},{65,97},{97,65},{2,34}... | collective-permute-start | bytes 786440 | tf_op jit(solution)/shard_map/ppermute | solution.py:383
  20.6 11.6 %collective-permute-start.3 = (f32[8,64,128]{2,1,0:T(8,128)S(1)}, f32[8,64,128]{2,1,0:T(8,128)S(1)}, u32[]{:S(2)}, u32[]{:S(2)}) collective-permute-start(f32[8,64,128]{2,1,0:T(8,128)S(1)} %get-tuple-element.25), channel_id=1, source_target_pairs={{0,96},{32,64},{64,32},{96,0},{1,97},{33,65},{65,33},{97,1},{2,98}... | collective-permute-start | bytes 786440 | tf_op jit(solution)/shard_map/ppermute | solution.py:383
  23.2 3.9 %collective-permute-start.4 = (f32[64,128]{1,0:T(8,128)S(1)}, f32[64,128]{1,0:T(8,128)S(1)}, u32[]{:S(2)}, u32[]{:S(2)}) collective-permute-start(f32[64,128]{1,0:T(8,128)S(1)} %get-tuple-element.26), channel_id=1, source_target_pairs={{0,8},{8,0},{16,24},{24,16},{1,9},{9,1},{17,25},{25,17},{2,10},{10... | collective-permute-start | bytes 98312 | tf_op jit(solution)/shard_map/ppermute | solution.py:383
  27.1 5.1 %collective-permute-start.5 = (f32[64,128]{1,0:T(8,128)S(1)}, f32[64,128]{1,0:T(8,128)S(1)}, u32[]{:S(2)}, u32[]{:S(2)}) collective-permute-start(f32[64,128]{1,0:T(8,128)S(1)} %get-tuple-element.27), channel_id=1, source_target_pairs={{0,24},{8,16},{16,8},{24,0},{1,25},{9,17},{17,9},{25,1},{2,26},{10... | collective-permute-start | bytes 98312 | tf_op jit(solution)/shard_map/ppermute | solution.py:383
  38.4 1.3 %collective-permute-start.6 = (f32[216,128]{1,0:T(8,128)S(1)}, f32[216,128]{1,0:T(8,128)S(1)}, u32[]{:S(2)}, u32[]{:S(2)}) collective-permute-start(f32[216,128]{1,0:T(8,128)S(1)} %get-tuple-element.29), channel_id=1, source_target_pairs={{0,1},{1,0},{2,3},{3,2},{4,5},{5,4},{6,7},{7,6},{8,9},{9,8},{10,11... | collective-permute-start | bytes 331784 | tf_op jit(solution)/shard_map/ppermute | solution.py:18
  39.8 8.8 %collective-permute-start.9 = (f32[216,128]{1,0:T(8,128)S(1)}, f32[216,128]{1,0:T(8,128)S(1)}, u32[]{:S(2)}, u32[]{:S(2)}) collective-permute-start(f32[216,128]{1,0:T(8,128)S(1)} %add.30), channel_id=1, source_target_pairs={{0,6},{1,7},{2,4},{3,5},{4,2},{5,3},{6,0},{7,1},{8,14},{9,15},{10,... | collective-permute-start | bytes 331784 | tf_op jit(solution)/shard_map/ppermute | solution.py:18
  40.7 7.9 %collective-permute-start.8 = (f32[216,128]{1,0:T(8,128)S(1)}, f32[216,128]{1,0:T(8,128)S(1)}, u32[]{:S(2)}, u32[]{:S(2)}) collective-permute-start(f32[216,128]{1,0:T(8,128)S(1)} %add.30), channel_id=1, source_target_pairs={{0,4},{1,5},{2,6},{3,7},{4,0},{5,1},{6,2},{7,3},{8,12},{9,13},{10,... | collective-permute-start | bytes 331784 | tf_op jit(solution)/shard_map/ppermute | solution.py:18
  41.2 7.9 %collective-permute-start.7 = (f32[216,128]{1,0:T(8,128)S(1)}, f32[216,128]{1,0:T(8,128)S(1)}, u32[]{:S(2)}, u32[]{:S(2)}) collective-permute-start(f32[216,128]{1,0:T(8,128)S(1)} %add.30), channel_id=1, source_target_pairs={{0,2},{1,3},{2,0},{3,1},{4,6},{5,7},{6,4},{7,5},{8,10},{9,11},{10,... | collective-permute-start | bytes 331784 | tf_op jit(solution)/shard_map/ppermute | solution.py:18
  49.2 7.2 %collective-permute-start.12 = (f32[216,128]{1,0:T(8,128)S(1)}, f32[216,128]{1,0:T(8,128)S(1)}, u32[]{:S(2)}, u32[]{:S(2)}) collective-permute-start(f32[216,128]{1,0:T(8,128)S(1)} %add_add_fusion.2), channel_id=1, source_target_pairs={{0,24},{8,16},{16,8},{24,0},{1,25},{9,17},{17,9},{25,1},{2,26},{10... | collective-permute-start | bytes 331784 | tf_op jit(solution)/shard_map/ppermute | solution.py:18
  52.3 6.4 %collective-permute-start.11 = (f32[216,128]{1,0:T(8,128)S(1)}, f32[216,128]{1,0:T(8,128)S(1)}, u32[]{:S(2)}, u32[]{:S(2)}) collective-permute-start(f32[216,128]{1,0:T(8,128)S(1)} %add_add_fusion.2), channel_id=1, source_target_pairs={{0,16},{8,24},{16,0},{24,8},{1,17},{9,25},{17,1},{25,9},{2,18},{10... | collective-permute-start | bytes 331784 | tf_op jit(solution)/shard_map/ppermute | solution.py:18
  52.3 6.4 %collective-permute-start.10 = (f32[216,128]{1,0:T(8,128)S(1)}, f32[216,128]{1,0:T(8,128)S(1)}, u32[]{:S(2)}, u32[]{:S(2)}) collective-permute-start(f32[216,128]{1,0:T(8,128)S(1)} %add_add_fusion.2), channel_id=1, source_target_pairs={{0,8},{8,0},{16,24},{24,16},{1,9},{9,1},{17,25},{25,17},{2,10},{10... | collective-permute-start | bytes 331784 | tf_op jit(solution)/shard_map/ppermute | solution.py:18
  58.7 7.2 %collective-permute-start.15 = (f32[216,128]{1,0:T(8,128)S(1)}, f32[216,128]{1,0:T(8,128)S(1)}, u32[]{:S(2)}, u32[]{:S(2)}) collective-permute-start(f32[216,128]{1,0:T(8,128)S(1)} %add_add_fusion.1), channel_id=1, source_target_pairs={{0,96},{32,64},{64,32},{96,0},{1,97},{33,65},{65,33},{97,1},{2,98}... | collective-permute-start | bytes 331784 | tf_op jit(solution)/shard_map/ppermute | solution.py:18
  59.5 6.4 %collective-permute-start.14 = (f32[216,128]{1,0:T(8,128)S(1)}, f32[216,128]{1,0:T(8,128)S(1)}, u32[]{:S(2)}, u32[]{:S(2)}) collective-permute-start(f32[216,128]{1,0:T(8,128)S(1)} %add_add_fusion.1), channel_id=1, source_target_pairs={{0,64},{32,96},{64,0},{96,32},{1,65},{33,97},{65,1},{97,33},{2,66}... | collective-permute-start | bytes 331784 | tf_op jit(solution)/shard_map/ppermute | solution.py:18
  61.9 4.9 %collective-permute-start.13 = (f32[216,128]{1,0:T(8,128)S(1)}, f32[216,128]{1,0:T(8,128)S(1)}, u32[]{:S(2)}, u32[]{:S(2)}) collective-permute-start(f32[216,128]{1,0:T(8,128)S(1)} %add_add_fusion.1), channel_id=1, source_target_pairs={{0,32},{32,0},{64,96},{96,64},{1,33},{33,1},{65,97},{97,65},{2,34}... | collective-permute-start | bytes 331784 | tf_op jit(solution)/shard_map/ppermute | solution.py:18
  66.8 1.6 %collective-permute-start.16 = (f32[216,128]{1,0:T(8,128)S(1)}, f32[216,128]{1,0:T(8,128)S(1)}, u32[]{:S(2)}, u32[]{:S(2)}) collective-permute-start(f32[216,128]{1,0:T(8,128)S(1)} %add_add_fusion.part), channel_id=1, source_target_pairs={{0,1},{1,0},{2,3},{3,2},{4,5},{5,4},{6,7},{7,6},{8,9},{9,8},{10,11... | collective-permute-start | bytes 331784 | tf_op jit(solution)/shard_map/ppermute | solution.py:18
